TPU v7x, 128 devices: a whole 4x4x4 slice. The times are simulated.
128 devices in a mesh: vintage: 2 (over core), tile: 64 (over x, y, z).
Axes of the slice: x: 4, y: 4, z: 4, core: 2. Of those that a mesh axis runs over, the one named last changes fastest.
Arguments:
- patches: bfloat16 [2, 32768, 768], P('vintage', 'tile'), may hold values from -16 to 16, as said below
- out_grad: bfloat16 [2, 32768, 768], P('vintage', 'tile'), may hold values from -6 to 6
- w_query: bfloat16 [768, 768], replicated, may hold values from -0.21875 to 0.21875
- w_key: bfloat16 [768, 256], replicated, may hold values from -0.21875 to 0.21875
- w_value: bfloat16 [768, 256], replicated, may hold values from -0.21875 to 0.21875
- w_out: bfloat16 [768, 768], replicated, may hold values from -0.21875 to 0.21875
- key_tiles: int32 [2, 256, 16], P('vintage'), may hold values from 0 to 63, all different within a row; in each aligned block of 4 rows (0 to 3, 4 to 7, ..., all dimensions but the last counted through in order) at most 2 rows name the same one
- key_blocks: int32 [2, 256, 16], P('vintage'), may hold values from 0 to 3
Outputs:
- layer_out: bfloat16 [2, 32768, 768], P('vintage', 'tile')
- input_grad: bfloat16 [2, 32768, 768], P('vintage', 'tile')
Inputs may be any that keep to these rules, and one draw needn't show every extreme that they name: `patches`: patch features of order one, rows of differing scale possible. `key_tiles`: the 16 tiles of one query block's list differ; over the 4 query blocks of one tile no key tile is named more than 2 times, and in every draw some tile is named exactly 2 times by some tile's blocks.
All inputs are finite; a program needn't handle non-finite values.
Results may differ from a plain program's by a relative error of at most 0.012.
The roundings to bfloat16 on the way count: a program that leaves them out, or rounds other values in their place, can miss the bound.
Values may be sent and summed in bfloat16 or wider, within the bound.
A program may use at most 128 MiB of HBM per device.

v0:
```python
import jax
import jax.numpy as jnp
from jax import lax
from jax.sharding import PartitionSpec as P

HEADS = 12
KV_HEADS = 4
HEAD_DIM = 64
BLK = 128
CAP = 2


EPSILON = 1e-06


def from_partner(value, axis, bit):
    return lax.ppermute(value, axis, [(i, i ^ 1 << bit) for i in range(lax.axis_size(axis))])


def block_work(query_rows, grad_rows, key_value, w_out):
    kv_width = KV_HEADS * HEAD_DIM
    group_size = HEADS // KV_HEADS
    temper = HEAD_DIM ** (-0.5)
    row_count = query_rows.shape[0]
    keys_low = key_value[:, :kv_width].reshape(-1, KV_HEADS, HEAD_DIM)
    values_low = key_value[:, kv_width:].reshape(-1, KV_HEADS, HEAD_DIM)
    query_low = query_rows.reshape(row_count, KV_HEADS, group_size, HEAD_DIM)
    scores = (
        jnp.einsum("igrd,ngd->grin", query_low, keys_low, preferred_element_type=jnp.float32)
        * temper
    )
    peak = jnp.max(scores, axis=-1, keepdims=True)
    expo = jnp.exp(scores - peak)
    probs = expo / jnp.sum(expo, axis=-1, keepdims=True)
    probs_low = probs.astype(jnp.bfloat16)
    attended = jnp.einsum(
        "grin,ngd->igrd", probs_low, values_low, preferred_element_type=jnp.float32
    )
    attended = attended.reshape(row_count, HEADS * HEAD_DIM).astype(jnp.bfloat16)
    attended_f = attended.astype(jnp.float32)
    root_mean = jnp.sqrt(jnp.mean(attended_f * attended_f, axis=-1, keepdims=True) + EPSILON)
    normed = attended_f / root_mean
    layer_rows = jnp.dot(
        normed.astype(jnp.bfloat16), w_out, preferred_element_type=jnp.float32
    ).astype(jnp.bfloat16)
    normed_grad = jnp.dot(grad_rows, w_out.T, preferred_element_type=jnp.float32)
    attended_grad = (
        normed_grad - normed * jnp.mean(normed_grad * normed, axis=-1, keepdims=True)
    ) / root_mean
    attended_grad = attended_grad.astype(jnp.bfloat16).reshape(
        row_count, KV_HEADS, group_size, HEAD_DIM
    )
    prob_grad = jnp.einsum(
        "igrd,ngd->grin", attended_grad, values_low, preferred_element_type=jnp.float32
    )
    row_dot = jnp.sum(probs * prob_grad, axis=-1, keepdims=True)
    score_grad = (probs * (prob_grad - row_dot) * temper).astype(jnp.bfloat16)
    query_grad = jnp.einsum(
        "grin,ngd->igrd", score_grad, keys_low, preferred_element_type=jnp.float32
    )
    query_grad = query_grad.reshape(row_count, HEADS * HEAD_DIM).astype(jnp.bfloat16)
    key_part = jnp.einsum(
        "grin,igrd->ngd", score_grad, query_low, preferred_element_type=jnp.float32
    )
    value_part = jnp.einsum(
        "grin,igrd->ngd", probs_low, attended_grad, preferred_element_type=jnp.float32
    )
    parts = jnp.concatenate(
        [key_part.reshape(-1, kv_width), value_part.reshape(-1, kv_width)], axis=-1
    )
    return (layer_rows, query_grad, parts.astype(jnp.bfloat16).reshape(-1, row_count, 2 * kv_width))


def slot_index(entry_tiles, tile_count):
    one_hot = (entry_tiles[:, None] == jnp.arange(tile_count, dtype=jnp.int32)[None, :]).astype(
        jnp.int32
    )
    ranks = jnp.cumsum(one_hot, axis=0) - 1
    return jnp.sum(one_hot * ranks, axis=1)


def shards(patches, out_grad, w_query, w_key, w_value, w_out, key_tiles, key_blocks):
    tokens = patches[0]
    grads_in = out_grad[0]
    kv_width = KV_HEADS * HEAD_DIM
    tile_count = lax.axis_size("tile")
    my_tile = lax.axis_index("tile")
    block_count = tokens.shape[0] // BLK
    list_len = key_tiles.shape[2]
    entry_count = block_count * list_len
    queries = jnp.dot(tokens, w_query, preferred_element_type=jnp.float32).astype(jnp.bfloat16)
    keys = jnp.dot(tokens, w_key, preferred_element_type=jnp.float32).astype(jnp.bfloat16)
    values = jnp.dot(tokens, w_value, preferred_element_type=jnp.float32).astype(jnp.bfloat16)
    local_kv = jnp.concatenate([keys, values], axis=-1)
    partner = from_partner(local_kv, "vintage", 0)
    partner_blocks = partner.reshape(block_count, BLK, 2 * kv_width)
    my_tiles = lax.dynamic_slice_in_dim(
        key_tiles[0], my_tile * block_count, block_count, 0
    ).reshape(-1)
    my_blocks = lax.dynamic_slice_in_dim(
        key_blocks[0], my_tile * block_count, block_count, 0
    ).reshape(-1)
    my_slots = slot_index(my_tiles, tile_count)
    flat_slot = my_tiles * CAP + my_slots
    tile_range = jnp.arange(tile_count, dtype=jnp.int32)
    slot_range = jnp.arange(CAP, dtype=jnp.int32)
    hits = (my_tiles[:, None, None] == tile_range[None, :, None]) & (
        my_slots[:, None, None] == slot_range[None, None, :]
    )
    table = jnp.sum(jnp.where(hits, my_blocks[:, None, None] + 1, 0), axis=0) - 1
    wanted = lax.all_to_all(table, "tile", split_axis=0, concat_axis=0, tiled=True)
    picked = partner_blocks[jnp.clip(wanted, 0, block_count - 1)]
    send_kv = jnp.where((wanted >= 0)[:, :, None, None], picked, jnp.zeros_like(picked))
    arrived = lax.all_to_all(send_kv, "tile", split_axis=0, concat_axis=0, tiled=True)
    entries = arrived.reshape(tile_count * CAP, BLK, 2 * kv_width)[flat_slot]
    entries = entries.reshape(block_count, list_len * BLK, 2 * kv_width)

    def per_block(item):
        query_rows, grad_rows, key_value = item
        return block_work(query_rows, grad_rows, key_value, w_out)

    layer_rows, query_grad, parts = lax.map(
        per_block,
        (
            queries.reshape(block_count, BLK, HEADS * HEAD_DIM),
            grads_in.reshape(block_count, BLK, tokens.shape[1]),
            entries,
        ),
    )
    parts = parts.reshape(entry_count, BLK, 2 * kv_width)
    back_send = (
        jnp.zeros((tile_count * CAP, BLK, 2 * kv_width), jnp.bfloat16).at[flat_slot].set(parts)
    )
    returned = lax.all_to_all(
        back_send.reshape(tile_count, CAP, BLK, 2 * kv_width),
        "tile",
        split_axis=0,
        concat_axis=0,
        tiled=True,
    )
    owner_hot = (
        wanted.reshape(-1)[:, None] == jnp.arange(block_count, dtype=jnp.int32)[None, :]
    ).astype(jnp.bfloat16)
    summed = jnp.einsum(
        "sj,snf->jnf",
        owner_hot,
        returned.reshape(tile_count * CAP, BLK, 2 * kv_width),
        preferred_element_type=jnp.float32,
    )
    kv_grad = summed.astype(jnp.bfloat16).reshape(tokens.shape[0], 2 * kv_width)
    away_term = jnp.dot(
        kv_grad[:, :kv_width], w_key.T, preferred_element_type=jnp.float32
    ) + jnp.dot(kv_grad[:, kv_width:], w_value.T, preferred_element_type=jnp.float32)
    kv_term = from_partner(away_term.astype(jnp.bfloat16), "vintage", 0).astype(away_term.dtype)
    query_rows_all = query_grad.reshape(tokens.shape[0], HEADS * HEAD_DIM)
    input_grad = (
        jnp.dot(query_rows_all, w_query.T, preferred_element_type=jnp.float32) + kv_term
    ).astype(jnp.bfloat16)
    layer_out = layer_rows.reshape(tokens.shape[0], tokens.shape[1])
    return (layer_out[None], input_grad[None])


def solution(mesh):
    in_specs = (
        P("vintage", "tile", None),
        P("vintage", "tile", None),
        P(),
        P(),
        P(),
        P(),
        P("vintage", None, None),
        P("vintage", None, None),
    )
    out_specs = (P("vintage", "tile", None), P("vintage", "tile", None))
    return jax.shard_map(shards, mesh=mesh, in_specs=in_specs, out_specs=out_specs, check_vma=False)
```

profile of v0, /device:TPU:127, one launch (start us, length us, event | category | flops | bytes accessed | tf_op | source)
XLA Modules:
  0.0 1125.3 jit_solution(17799416571803076304)
XLA Ops:
  3.1 9.5 all-to-all-start
  26.9 14.0 %broadcast_select_fusion = bf16[64,2,128,512]{3,2,1,0:T(8,128)(2,1)} fusion(bf16[64,2,128,512]{3,2,1,0:T(8,128)(2,1)} %bitcast.223, pred[64,2]{1,0:T(8,128)(4,1)S(1)} %copy.101), kind=kLoop, calls=%fused_computation.56 | loop fusion | flops 8388608 | bytes 33554560 | tf_op jit(solution)/shard_map/jit(_where)/select_n | solution.py:113
  40.8 10.2 all-to-all-start.1
  53.4 253.3 %all-to-all-done.1 = bf16[64,2,128,512]{3,2,1,0:T(8,128)(2,1)} async-done(((bf16[64,2,128,512]{3,2,1,0:T(8,128)(2,1)}), bf16[64,2,128,512]{3,2,1,0:T(8,128)(2,1)}, u32[]{:S(2)}, u32[]{:S(2)}) %all-to-all-start.1) | async-done | bytes 16777248 | tf_op jit(solution)/shard_map/all_to_all | solution.py:114
  306.7 11.3 %gather_fusion.1 = bf16[64,128,512]{2,1,0:T(8,128)(2,1)} fusion(bf16[128,128,512]{2,1,0:T(8,128)(2,1)} %bitcast.33, s32[1024]{0:T(1024)S(1)} %pad_clamp_fusion), kind=kCustom, calls=%fused_computation.1 | custom fusion | bytes 16777472 | tf_op jit(solution)/shard_map/gather | solution.py:115
  318.0 351.0 %while.14 = (s32[]{:T(128)}, bf16[4,128,768]{2,1,0:T(8,128)(2,1)}, bf16[4,128,768]{2,1,0:T(8,128)(2,1)}, bf16[4,16,128,512]{3,2,1,0:T(8,128)(2,1)}, bf16[4,2048,...) while((s32[]{:T(128)}, bf16[4,128,768]{2,1,0:T(8,128)(2,1)}, ...), condition=%wide.region_9.10_spmd, body=%wide.region_3.9_spmd.sunk | while | flops 2787648512 | bytes 156142864 | solution.py:122
  326.7 9.7 fusion.114
  354.9 19.3 %fusion.117 = bf16[4,64,3,128]{3,1,2,0:T(8,128)(2,1)S(1)} fusion(bf16[2048,4,64,1]{0,2,3,1:T(8,128)(2,1)S(1)} %bitcast.228, f32[4,2048,128,3]{2,1,3,0:T(8,128)} %fusion.116, f32[4,3,128,2048]{2,3,1,0:T(8,128)} %get-tuple-element.176, f32[4,3,128]{2,1,0:T(4,128)S(1)} %get-tuple-element.177), kind=kOutput, calls=%fused_computation.32.clone.1 | convolution fusion | flops 424775168 | bytes 26417152 | tf_op jit(solution)/shard_map/while/body/eval_jaxpr/grin,ngd->igrd/dot_general | solution.py:58
  382.1 17.3 %fusion.119 = bf16[4,64,2048]{2,1,0:T(8,128)(2,1)S(1)} fusion(bf16[128,4,3,64]{0,3,2,1:T(8,128)(2,1)S(1)} %bitcast.234, f32[4,2048,128,3]{2,1,3,0:T(8,128)} %fusion.116, f32[4,3,128,2048]{2,3,1,0:T(8,128)} %get-tuple-element.176, f32[4,3,128]{2,1,0:T(4,128)S(1)} %get-tuple-element.177), kind=kOutput, calls=%fused_computation.27.clone.1 | convolution fusion | flops 425201152 | bytes 26417152 | tf_op jit(solution)/shard_map/while/body/eval_jaxpr/grin,igrd->ngd/dot_general | solution.py:62
  414.5 9.7 fusion.114
  442.7 19.3 %fusion.117 = bf16[4,64,3,128]{3,1,2,0:T(8,128)(2,1)S(1)} fusion(bf16[2048,4,64,1]{0,2,3,1:T(8,128)(2,1)S(1)} %bitcast.228, f32[4,2048,128,3]{2,1,3,0:T(8,128)} %fusion.116, f32[4,3,128,2048]{2,3,1,0:T(8,128)} %get-tuple-element.176, f32[4,3,128]{2,1,0:T(4,128)S(1)} %get-tuple-element.177), kind=kOutput, calls=%fused_computation.32.clone.1 | convolution fusion | flops 424775168 | bytes 26417152 | tf_op jit(solution)/shard_map/while/body/eval_jaxpr/grin,ngd->igrd/dot_general | solution.py:58
  469.8 17.3 %fusion.119 = bf16[4,64,2048]{2,1,0:T(8,128)(2,1)S(1)} fusion(bf16[128,4,3,64]{0,3,2,1:T(8,128)(2,1)S(1)} %bitcast.234, f32[4,2048,128,3]{2,1,3,0:T(8,128)} %fusion.116, f32[4,3,128,2048]{2,3,1,0:T(8,128)} %get-tuple-element.176, f32[4,3,128]{2,1,0:T(4,128)S(1)} %get-tuple-element.177), kind=kOutput, calls=%fused_computation.27.clone.1 | convolution fusion | flops 425201152 | bytes 26417152 | tf_op jit(solution)/shard_map/while/body/eval_jaxpr/grin,igrd->ngd/dot_general | solution.py:62
  502.3 9.7 fusion.114
  530.5 19.3 %fusion.117 = bf16[4,64,3,128]{3,1,2,0:T(8,128)(2,1)S(1)} fusion(bf16[2048,4,64,1]{0,2,3,1:T(8,128)(2,1)S(1)} %bitcast.228, f32[4,2048,128,3]{2,1,3,0:T(8,128)} %fusion.116, f32[4,3,128,2048]{2,3,1,0:T(8,128)} %get-tuple-element.176, f32[4,3,128]{2,1,0:T(4,128)S(1)} %get-tuple-element.177), kind=kOutput, calls=%fused_computation.32.clone.1 | convolution fusion | flops 424775168 | bytes 26417152 | tf_op jit(solution)/shard_map/while/body/eval_jaxpr/grin,ngd->igrd/dot_general | solution.py:58
  557.6 17.3 %fusion.119 = bf16[4,64,2048]{2,1,0:T(8,128)(2,1)S(1)} fusion(bf16[128,4,3,64]{0,3,2,1:T(8,128)(2,1)S(1)} %bitcast.234, f32[4,2048,128,3]{2,1,3,0:T(8,128)} %fusion.116, f32[4,3,128,2048]{2,3,1,0:T(8,128)} %get-tuple-element.176, f32[4,3,128]{2,1,0:T(4,128)S(1)} %get-tuple-element.177), kind=kOutput, calls=%fused_computation.27.clone.1 | convolution fusion | flops 425201152 | bytes 26417152 | tf_op jit(solution)/shard_map/while/body/eval_jaxpr/grin,igrd->ngd/dot_general | solution.py:62
  590.0 9.7 fusion.114
  618.2 19.3 %fusion.117 = bf16[4,64,3,128]{3,1,2,0:T(8,128)(2,1)S(1)} fusion(bf16[2048,4,64,1]{0,2,3,1:T(8,128)(2,1)S(1)} %bitcast.228, f32[4,2048,128,3]{2,1,3,0:T(8,128)} %fusion.116, f32[4,3,128,2048]{2,3,1,0:T(8,128)} %get-tuple-element.176, f32[4,3,128]{2,1,0:T(4,128)S(1)} %get-tuple-element.177), kind=kOutput, calls=%fused_computation.32.clone.1 | convolution fusion | flops 424775168 | bytes 26417152 | tf_op jit(solution)/shard_map/while/body/eval_jaxpr/grin,ngd->igrd/dot_general | solution.py:58
  645.4 17.3 %fusion.119 = bf16[4,64,2048]{2,1,0:T(8,128)(2,1)S(1)} fusion(bf16[128,4,3,64]{0,3,2,1:T(8,128)(2,1)S(1)} %bitcast.234, f32[4,2048,128,3]{2,1,3,0:T(8,128)} %fusion.116, f32[4,3,128,2048]{2,3,1,0:T(8,128)} %get-tuple-element.176, f32[4,3,128]{2,1,0:T(4,128)S(1)} %get-tuple-element.177), kind=kOutput, calls=%fused_computation.27.clone.1 | convolution fusion | flops 425201152 | bytes 26417152 | tf_op jit(solution)/shard_map/while/body/eval_jaxpr/grin,igrd->ngd/dot_general | solution.py:62
  674.9 22.1 %scatter_fusion = bf16[128,128,512]{2,1,0:T(8,128)(2,1)} fusion(bf16[128,128,512]{2,1,0:T(8,128)(2,1)} %broadcast_in_dim.58, s32[64]{0:T(128)S(1)} %copy-done.12, bf16[64,128,512]{2,1,0:T(8,128)(2,1)} %bitcast.232), kind=kCustom, calls=%fused_computation.2 | custom fusion | bytes 25166080 | tf_op jit(solution)/shard_map/scatter | solution.py:132
  697.0 30.7 %copy.110 = bf16[64,2,128,512]{3,1,2,0:T(2,128)(2,1)} copy(bf16[64,2,128,512]{3,2,1,0:T(8,128)(2,1)} %bitcast.218) | data formatting | bytes 33554432 | tf_op jit(solution)/shard_map/reshape | solution.py:135
  727.7 46.8 %all-to-all-start.2 = ((bf16[64,2,128,512]{3,1,2,0:T(2,128)(2,1)}), bf16[64,2,128,512]{3,1,2,0:T(2,128)(2,1)}, u32[]{:S(2)}, u32[]{:S(2)}) async-start(bf16[64,2,128,512]{3,1,2,0:T(2,128)(2,1)} %copy.110), calls=%async_computation.2 | async-start | bytes 33554432 | tf_op jit(solution)/shard_map/all_to_all | solution.py:134
  776.0 295.9 %all-to-all-done.2 = bf16[64,2,128,512]{3,1,2,0:T(2,128)(2,1)} async-done(((bf16[64,2,128,512]{3,1,2,0:T(2,128)(2,1)}), bf16[64,2,128,512]{3,1,2,0:T(2,128)(2,1)}, u32[]{:S(2)}, u32[]{:S(2)}) %all-to-all-start.2) | async-done | bytes 16777248 | tf_op jit(solution)/shard_map/all_to_all | solution.py:134
  1071.9 14.4 %copy.111 = bf16[64,2,128,512]{3,1,0,2:T(2,128)(2,1)} copy(bf16[64,2,128,512]{3,1,2,0:T(2,128)(2,1)} %all-to-all-done.2) | data formatting | bytes 33554432 | tf_op jit(solution)/shard_map/all_to_all | solution.py:134
  1086.3 24.9 %reshape.255 = bf16[128,128,512]{2,0,1:T(8,128)(2,1)} reshape(bf16[64,2,128,512]{3,1,0,2:T(2,128)(2,1)} %copy.111) | data formatting | bytes 33554432 | tf_op jit(solution)/shard_map/reshape | solution.py:147
  (192 shorter events, 205.4 us)
Async XLA Ops:
  0.6 51.0 %copy-start = (bf16[768,768]{1,0:T(8,128)(2,1)S(1)}, bf16[768,768]{1,0:T(8,128)(2,1)}, u32[]{:S(2)}) copy-start(bf16[768,768]{1,0:T(8,128)(2,1)} %param.12) | copy-start | bytes 3538948
  3.1 14.2 %all-to-all-start = ((s32[64,1,2]{2,1,0:T(1,128)}), s32[64,1,2]{2,1,0:T(1,128)S(1)}, u32[]{:S(2)}, u32[]{:S(2)}) async-start(s32[64,1,2]{2,1,0:T(1,128)} %copy.99), calls=%async_computation | async-start | bytes 65536 | tf_op jit(solution)/shard_map/all_to_all | solution.py:111
  15.9 2.9 collective-permute-start
  40.8 10.9 copy-start.6
  40.8 265.9 %all-to-all-start.1 = ((bf16[64,2,128,512]{3,2,1,0:T(8,128)(2,1)}), bf16[64,2,128,512]{3,2,1,0:T(8,128)(2,1)}, u32[]{:S(2)}, u32[]{:S(2)}) async-start(bf16[64,2,128,512]{3,2,1,0:T(8,128)(2,1)} %broadcast_select_fusion), calls=%async_computation.1 | async-start | bytes 33554432 | tf_op jit(solution)/shard_map/all_to_all | solution.py:114
  325.5 11.0 copy-start.1
  326.7 15.4 %copy-start.4 = (bf16[1,128,768]{1,2,0:T(8,128)(2,1)}, bf16[1,128,768]{1,2,0:T(8,128)(2,1)S(1)}, u32[]{:S(2)}) copy-start(bf16[1,128,768]{1,2,0:T(8,128)(2,1)S(1)} %copy.142) | copy-start | bytes 589828 | tf_op jit(solution)/shard_map/while
  346.9 8.1 copy-start.2
  354.9 20.2 %copy-start.3 = (bf16[128,768]{0,1:T(8,128)(2,1)S(1)}, bf16[128,768]{0,1:T(8,128)(2,1)}, u32[]{:S(2)}) copy-start(bf16[128,768]{0,1:T(8,128)(2,1)} %copy.144) | copy-start | bytes 589828 | tf_op jit(solution)/shard_map/while
  413.3 11.0 copy-start.1
  414.5 15.4 %copy-start.4 = (bf16[1,128,768]{1,2,0:T(8,128)(2,1)}, bf16[1,128,768]{1,2,0:T(8,128)(2,1)S(1)}, u32[]{:S(2)}) copy-start(bf16[1,128,768]{1,2,0:T(8,128)(2,1)S(1)} %copy.142) | copy-start | bytes 589828 | tf_op jit(solution)/shard_map/while
  442.7 20.2 %copy-start.3 = (bf16[128,768]{0,1:T(8,128)(2,1)S(1)}, bf16[128,768]{0,1:T(8,128)(2,1)}, u32[]{:S(2)}) copy-start(bf16[128,768]{0,1:T(8,128)(2,1)} %copy.144) | copy-start | bytes 589828 | tf_op jit(solution)/shard_map/while
  501.1 11.0 copy-start.1
  502.3 15.4 %copy-start.4 = (bf16[1,128,768]{1,2,0:T(8,128)(2,1)}, bf16[1,128,768]{1,2,0:T(8,128)(2,1)S(1)}, u32[]{:S(2)}) copy-start(bf16[1,128,768]{1,2,0:T(8,128)(2,1)S(1)} %copy.142) | copy-start | bytes 589828 | tf_op jit(solution)/shard_map/while
  530.5 20.2 %copy-start.3 = (bf16[128,768]{0,1:T(8,128)(2,1)S(1)}, bf16[128,768]{0,1:T(8,128)(2,1)}, u32[]{:S(2)}) copy-start(bf16[128,768]{0,1:T(8,128)(2,1)} %copy.144) | copy-start | bytes 589828 | tf_op jit(solution)/shard_map/while
  588.8 11.0 copy-start.1
  590.0 15.4 %copy-start.4 = (bf16[1,128,768]{1,2,0:T(8,128)(2,1)}, bf16[1,128,768]{1,2,0:T(8,128)(2,1)S(1)}, u32[]{:S(2)}) copy-start(bf16[1,128,768]{1,2,0:T(8,128)(2,1)S(1)} %copy.142) | copy-start | bytes 589828 | tf_op jit(solution)/shard_map/while
  618.2 20.2 %copy-start.3 = (bf16[128,768]{0,1:T(8,128)(2,1)S(1)}, bf16[128,768]{0,1:T(8,128)(2,1)}, u32[]{:S(2)}) copy-start(bf16[128,768]{0,1:T(8,128)(2,1)} %copy.144) | copy-start | bytes 589828 | tf_op jit(solution)/shard_map/while
  727.7 47.4 %copy-start.10 = (s32[64,1,2]{2,1,0:T(1,128)S(1)}, s32[64,1,2]{2,1,0:T(1,128)}, u32[]{:S(2)}) copy-start(s32[64,1,2]{2,1,0:T(1,128)} %copy-done.9) | copy-start | bytes 1540
  727.7 344.2 %all-to-all-start.2 = ((bf16[64,2,128,512]{3,1,2,0:T(2,128)(2,1)}), bf16[64,2,128,512]{3,1,2,0:T(2,128)(2,1)}, u32[]{:S(2)}, u32[]{:S(2)}) async-start(bf16[64,2,128,512]{3,1,2,0:T(2,128)(2,1)} %copy.110), calls=%async_computation.2 | async-start | bytes 33554432 | tf_op jit(solution)/shard_map/all_to_all | solution.py:134
  1111.1 8.3 copy-start.7
  1111.1 8.7 copy-start.8
  1111.1 12.5 %copy-start.13 = (bf16[4,128,768]{2,1,0:T(8,128)(2,1)S(1)}, bf16[4,128,768]{2,1,0:T(8,128)(2,1)}, u32[]{:S(2)}) copy-start(bf16[4,128,768]{2,1,0:T(8,128)(2,1)} %get-tuple-element.47) | copy-start | bytes 2359300
  1120.2 3.4 collective-permute-start.1
  (10 other events, 59.2 us)
where the time goes:
time: 1130 us
  waiting for transfers between devices  552 us (49%)
  matrix products  297 us (26%)
  local copies, waits for them, and re-layouts  183 us (16%)
  starting transfers between devices  69.2 us (6%)
  other arithmetic  22.9 us (2%)
    all_to_all x1, waiting for transfers between devices, shards(): lax.all_to_all(back_send.reshape(tile_count, CAP, BLK, 2 * kv_width), 'ti...  296 us
    all_to_all x1, waiting for transfers between devices, shards(): lax.all_to_all(send_kv, 'tile', split_axis=0, concat_axis=0, tiled=True)  253 us
    dot_general x4, matrix products, block_work(): jnp.einsum('grin,ngd->igrd', score_grad, keys_low, preferred_element_type...  77.3 us
    dot_general x4, matrix products, block_work(): jnp.einsum('grin,igrd->ngd', score_grad, query_low, preferred_element_typ...  69.3 us
    all_to_all x1, starting transfers between devices, shards(): lax.all_to_all(back_send.reshape(tile_count, CAP, BLK, 2 * kv_width), 'ti...  46.8 us
    sub x4, matrix products, block_work(): expo = jnp.exp(scores - peak)  39 us
    reshape x1, local copies, waits for them, and re-layouts, shards(): back_send.reshape(tile_count, CAP, BLK, 2 * kv_width)  30.7 us
    dot_general x4, matrix products, block_work(): jnp.einsum('igrd,ngd->grin', attended_grad, values_low, preferred_element...  28.9 us
  transfers between devices with their start and end apart: 5, of which 4 were waited for; matrix products, arithmetic and copies ran while one was open for 1% of the time, Pallas kernels for 0%

commit v1 on v0

v1 whole, which is shorter than its diff:
```python
import functools

import jax
import jax.numpy as jnp
from jax import lax
from jax.experimental import pallas as pl
from jax.experimental.pallas import tpu as pltpu
from jax.sharding import PartitionSpec as P

CAP = 2
LOG2E = 1.4426950408889634
EPSILON = 1e-06
F32, BF16 = jnp.float32, jnp.bfloat16

def swap_halves(x):
    return jnp.concatenate([x[:, 64:], x[:, :64]], axis=1)

def dot(a, b, ca=1, cb=0):
    return lax.dot_general(a, b, (((ca,), (cb,)), ((), ())), preferred_element_type=F32)

def attend_kernel(slots, q_ref, go_ref, wo_ref, arr_ref, lay_ref, dq_ref, out_ref,
                  kv, stage, qp, dop, p, t, acc, stat, att, in_sem, out_sem, *, NC1, NC2):
    b = pl.program_id(0)
    nb = pl.num_programs(0)
    L = kv.shape[1]

    def fetch(blk, slot):
        return [pltpu.make_async_copy(arr_ref.at[slots[blk * L + l]], kv.at[slot, l], in_sem.at[slot, l]) for l in range(L)]

    def put(blk, slot):
        return [pltpu.make_async_copy(stage.at[slot, l], out_ref.at[slots[blk * L + l]], out_sem.at[slot, l]) for l in range(L)]

    cur = lax.rem(b, 2)

    @pl.when(b == 0)
    def _():
        for c in fetch(0, 0):
            c.start()

    @pl.when(b + 1 < nb)
    def _():
        for c in fetch(b + 1, 1 - cur):
            c.start()

    low = lax.broadcasted_iota(jnp.int32, (128, 128), 1) < 64

    def pad_heads(src, dst):
        for h in range(12):
            g = h // 3
            tile = src[:, (h // 2) * 128:(h // 2) * 128 + 128]
            if h % 2 != g % 2:
                tile = swap_halves(tile)
            tile = jnp.where(low if g % 2 == 0 else ~low, tile, jnp.zeros_like(tile))
            dst[g // 2, ((g % 2) * 3 + h % 3) * 128:((g % 2) * 3 + h % 3) * 128 + 128, :] = tile.astype(BF16)

    def unpad(src, j):
        parts = []
        for h in (2 * j, 2 * j + 1):
            g = h // 3
            rows = ((g % 2) * 3 + h % 3) * 128
            tile = src[g // 2, rows:rows + 128, :]
            if h % 2 != g % 2:
                tile = swap_halves(tile)
            parts.append(tile)
        return jnp.where(low, parts[0], parts[1])

    pad_heads(q_ref[...].astype(F32), qp)
    for c in fetch(b, cur):
        c.wait()

    scale = 0.125 * LOG2E
    R = 768
    for c in range(2):
        def scores(n, m):
            e0 = n * (NC1 // 128)
            k = kv[cur, pl.ds(e0, NC1 // 128), c * 128:c * 128 + 128, :].reshape(NC1, 128)
            s = dot(qp[c], k, 1, 1)
            p[c, :, pl.ds(pl.multiple_of(n * NC1, 128), NC1)] = s
            for i in range(NC1 // 128):
                m = jnp.maximum(m, s[:, i * 128:i * 128 + 128])
            return m
        m = lax.fori_loop(0, 2048 // NC1, scores, jnp.full((R, 128), -jnp.inf, F32))
        stat[...] = jnp.broadcast_to(jnp.max(m, axis=1, keepdims=True), (R, 128))

        def expo(n, tot):
            cols = pl.ds(pl.multiple_of(n * NC1, 128), NC1)
            mm = stat[...]
            for i in range(NC1 // 128):
                cols = pl.ds(pl.multiple_of(n * NC1 + i * 128, 128), 128)
                e = jnp.exp2((p[c, :, cols] - mm) * scale)
                p[c, :, cols] = e
                tot = tot + e
            return tot
        tot = lax.fori_loop(0, 2048 // NC1, expo, jnp.zeros((R, 128), F32))
        stat[...] = jnp.broadcast_to(1.0 / jnp.sum(tot, axis=1, keepdims=True), (R, 128))
        acc[c] = jnp.zeros((R, 128), F32)

        def attend(n, _):
            inv = stat[...]
            e0 = n * (NC1 // 128)
            v = kv[cur, pl.ds(e0, NC1 // 128), 256 + c * 128:256 + c * 128 + 128, :].reshape(NC1, 128)
            pl_ = []
            for i in range(NC1 // 128):
                cols = pl.ds(pl.multiple_of(n * NC1 + i * 128, 128), 128)
                pr = p[c, :, cols] * inv
                p[c, :, cols] = pr
                pl_.append(pr.astype(BF16))
            acc[c] += dot(jnp.concatenate(pl_, axis=1), v)
            return 0
        lax.fori_loop(0, 2048 // NC1, attend, 0)

    ss = jnp.zeros((128, 128), F32)
    for j in range(6):
        a = unpad(acc, j).astype(BF16).astype(F32)
        att[:, j * 128:j * 128 + 128] = a
        ss = ss + a * a
    root = jnp.sqrt(jnp.sum(ss, axis=1, keepdims=True) * (1.0 / 768) + EPSILON)
    normed = att[...] / root
    lay_ref[...] = dot(normed.astype(BF16), wo_ref[...]).astype(BF16)
    ng = dot(go_ref[...], wo_ref[...], 1, 1)
    ag = (ng - normed * (jnp.sum(ng * normed, axis=1, keepdims=True) * (1.0 / 768))) / root
    pad_heads(ag.astype(BF16).astype(F32), dop)

    @pl.when(b >= 2)
    def _():
        for cp in put(b - 2, cur):
            cp.wait()

    for c in range(2):
        dos = (dop[c].astype(F32) * 0.125).astype(BF16)

        def pgrad(n, rd):
            e0 = n * (NC1 // 128)
            v = kv[cur, pl.ds(e0, NC1 // 128), 256 + c * 128:256 + c * 128 + 128, :].reshape(NC1, 128)
            dp = dot(dos, v, 1, 1)
            for i in range(NC1 // 128):
                cols = pl.ds(pl.multiple_of(n * NC1 + i * 128, 128), 128)
                x = dp[:, i * 128:i * 128 + 128] * p[c, :, cols]
                t[:, cols] = x
                rd = rd + x
            return rd
        rd = lax.fori_loop(0, 2048 // NC1, pgrad, jnp.zeros((R, 128), F32))
        stat[...] = jnp.broadcast_to(jnp.sum(rd, axis=1, keepdims=True), (R, 128))
        acc[c] = jnp.zeros((R, 128), F32)

        def grads(n, _):
            rdb = stat[...]
            e0 = n * (NC2 // 128)
            ne = NC2 // 128
            k = kv[cur, pl.ds(e0, ne), c * 128:c * 128 + 128, :].reshape(NC2, 128)
            ds_, pl_ = [], []
            for i in range(ne):
                cols = pl.ds(pl.multiple_of(n * NC2 + i * 128, 128), 128)
                pr = p[c, :, cols]
                ds_.append((t[:, cols] - pr * rdb).astype(BF16))
                pl_.append(pr.astype(BF16))
            ds_ = jnp.concatenate(ds_, axis=1)
            pl_ = jnp.concatenate(pl_, axis=1)
            acc[c] += dot(ds_, k)
            dk = dot(ds_, qp[c], 0, 0)
            dv = dot(pl_, dop[c], 0, 0)
            stage[cur, pl.ds(e0, ne), c * 128:c * 128 + 128, :] = dk.astype(BF16).reshape(ne, 128, 128)
            stage[cur, pl.ds(e0, ne), 256 + c * 128:256 + c * 128 + 128, :] = dv.astype(BF16).reshape(ne, 128, 128)
            return 0
        lax.fori_loop(0, 2048 // NC2, grads, 0)

    for j in range(6):
        dq_ref[:, j * 128:j * 128 + 128] = unpad(acc, j).astype(BF16)

    for cp in put(b, cur):
        cp.start()

    @pl.when(b == nb - 1)
    def _():
        for cp in put(b - 1, 1 - cur):
            cp.wait()
        for cp in put(b, cur):
            cp.wait()

def attention(slots, queries, grads, w_out, arr, NC1=256, NC2=256):
    rows, D = queries.shape
    nb = rows // 128
    L = slots.shape[0] // nb
    ns = arr.shape[0]
    row = lambda b, s: (b, 0)
    return pl.pallas_call(
        functools.partial(attend_kernel, NC1=NC1, NC2=NC2),
        grid_spec=pltpu.PrefetchScalarGridSpec(
            num_scalar_prefetch=1, grid=(nb,),
            in_specs=[pl.BlockSpec((128, D), row), pl.BlockSpec((128, D), row),
                      pl.BlockSpec((D, D), lambda b, s: (0, 0), pipeline_mode=pl.Buffered(1)),
                      pl.BlockSpec(memory_space=pl.ANY)],
            out_specs=[pl.BlockSpec((128, D), row), pl.BlockSpec((128, D), row), pl.BlockSpec(memory_space=pl.ANY)],
            scratch_shapes=[
                pltpu.VMEM((2, L, 512, 128), BF16), pltpu.VMEM((2, L, 512, 128), BF16),
                pltpu.VMEM((2, 768, 128), BF16), pltpu.VMEM((2, 768, 128), BF16),
                pltpu.VMEM((2, 768, 2048), F32), pltpu.VMEM((768, 2048), F32),
                pltpu.VMEM((2, 768, 128), F32), pltpu.VMEM((768, 128), F32), pltpu.VMEM((128, 768), F32),
                pltpu.SemaphoreType.DMA((2, L)), pltpu.SemaphoreType.DMA((2, L))]),
        out_shape=[jax.ShapeDtypeStruct((rows, D), BF16), jax.ShapeDtypeStruct((rows, D), BF16),
                   jax.ShapeDtypeStruct((ns, 512, 128), BF16)],
        compiler_params=pltpu.CompilerParams(dimension_semantics=("arbitrary",), vmem_limit_bytes=60 * 2**20),
        name="attend",
    )(slots, queries, grads, w_out, arr)


MESH = pl.DeviceIdType.MESH
SIDE = 4
ORDERS = ((0, 1, 2), (1, 2, 0), (2, 0, 1))
PIECES = ((0, 176), (176, 176), (352, 160))
STRIDE = (16, 4, 1)


def place():
    tile = lax.axis_index("tile")
    return [lax.rem(lax.div(tile, s), SIDE) for s in STRIDE]


def shifted(pos, axis, by):
    moved = list(pos)
    moved[axis] = lax.rem(pos[axis] + by, SIDE)
    return moved


def tile_of(pos):
    return pos[0] * 16 + pos[1] * 4 + pos[2]


def greet(pos, core):
    barrier = pltpu.get_barrier_semaphore()
    count = 0
    for axis in range(3):
        for by in (1, 3):
            pl.semaphore_signal(barrier, inc=1, device_id=(core, tile_of(shifted(pos, axis, by))), device_id_type=MESH)
            count += 1
    pl.semaphore_signal(barrier, inc=1, device_id=(1 - core, tile_of(pos)), device_id_type=MESH)
    pl.semaphore_wait(barrier, count + 1)


class Sender:
    def __init__(self, pos, core, send_sem, recv_sem):
        self.pos, self.core, self.send_sem, self.recv_sem = pos, core, send_sem, recv_sem
        self.done = []

    def copy(self, src, dst, sem, axis, by):
        c = pltpu.make_async_remote_copy(
            src_ref=src, dst_ref=dst, send_sem=self.send_sem.at[sem], recv_sem=self.recv_sem.at[sem],
            device_id=(self.core, tile_of(shifted(self.pos, axis, by))), device_id_type=MESH)
        c.start()
        self.done.append(c)
        return c


def at_axis(ref, dims, index, axis, *rest):
    return ref.at[tuple(index if d == axis else slice(None) for d in dims) + rest]


def spread_kernel(wanted, mine_ref, out_ref, own, plane0, plane1, plane2, st0, st1, st2, rl0, rl1, rl2,
                  send_sem, recv_sem, swap_sem, local_sem):
    pos, core = place(), lax.axis_index("vintage")
    planes, stages, relays = (plane0, plane1, plane2), (st0, st1, st2), (rl0, rl1, rl2)
    greet(pos, core)
    swap = pltpu.make_async_remote_copy(
        src_ref=mine_ref, dst_ref=own, send_sem=swap_sem.at[0], recv_sem=swap_sem.at[1],
        device_id=(1 - core, tile_of(pos)), device_id_type=MESH)
    swap.start()
    swap.wait()
    send = Sender(pos, core, send_sem, recv_sem)
    dims = [tuple(sorted(o[:2])) for o in ORDERS]
    local = []

    def line(p, axis):
        return at_axis(planes[p], dims[p], pos[axis], axis)

    def cell(p, a1, i1, a2, i2, *rest):
        return planes[p].at[tuple(i1 if d == a1 else i2 for d in dims[p]) + rest]

    for p, (r0, rows) in enumerate(PIECES):
        a1, a2, a3 = ORDERS[p]
        c = pltpu.make_async_copy(own.at[:, pl.ds(r0, rows), :], cell(p, a1, pos[a1], a2, pos[a2]), local_sem.at[p])
        c.start()
        local.append(c)
    first = []
    for p in range(3):
        a1, a2, a3 = ORDERS[p]
        local[p].wait()
        here = cell(p, a1, pos[a1], a2, pos[a2])
        first.append([send.copy(here, here, p * 12 + i, a1, by) for i, by in enumerate((1, 3))])
    second = []
    for p in range(3):
        a1, a2, a3 = ORDERS[p]
        got = []
        for i, by in enumerate((1, 3)):
            first[p][i].wait_recv()
            part = cell(p, a1, lax.rem(pos[a1] + SIDE - by, SIDE), a2, pos[a2], pl.ds(2 * i, 2))
            got.append(send.copy(part, part, p * 12 + 2 + i, a1, by))
        second.append(got)
    third = []
    for p in range(3):
        a1, a2, a3 = ORDERS[p]
        for c in second[p]:
            c.wait_recv()
        here = line(p, a2)
        third.append([send.copy(here, here, p * 12 + 4 + i, a2, by) for i, by in enumerate((1, 3))])
    fourth = []
    for p in range(3):
        a1, a2, a3 = ORDERS[p]
        got = []
        for i, by in enumerate((1, 3)):
            third[p][i].wait_recv()
            other = lax.rem(pos[a2] + SIDE - by, SIDE)
            part = planes[p].at[tuple(other if d == a2 else pl.ds(2 * i, 2) for d in dims[p])]
            got.append(send.copy(part, part, p * 12 + 6 + i, a2, by))
        fourth.append(got)

    def landing(p, source, half=None):
        a3 = ORDERS[p][2]
        r0, rows = PIECES[p]
        idx = []
        for d in range(3):
            if d == a3:
                idx.append(source)
            elif half is not None and d == dims[p][0]:
                idx.append(pl.ds(2 * half, 2))
            else:
                idx.append(slice(None))
        return out_ref.at[tuple(idx) + (slice(None), pl.ds(r0, rows), slice(None))]

    fifth = []
    for p in range(3):
        a1, a2, a3 = ORDERS[p]
        r0, rows = PIECES[p]
        for c in fourth[p]:
            c.wait_recv()

        def pick(k, by, p=p, a3=a3):
            dest = tile_of(shifted(pos, a3, by))

            def one(j, _):
                hi, lo = lax.div(j, SIDE), lax.rem(j, SIDE)
                source = pos[a3] * STRIDE[a3] + hi * STRIDE[dims[p][0]] + lo * STRIDE[dims[p][1]]
                for s in range(2):
                    blk = jnp.maximum(wanted[dest * 128 + s * 64 + source], 0)
                    stages[p][k, hi, lo, s] = planes[p][hi, lo, blk]
                return 0
            lax.fori_loop(0, SIDE * SIDE, one, 0)

        got = []
        pick(2, 2)
        for i, by in enumerate((1, 3)):
            got.append(send.copy(stages[p].at[2, pl.ds(2 * i, 2)], relays[p].at[i], p * 12 + 8 + i, a3, by))
        for i, by in enumerate((1, 3)):
            pick(i, by)
            send.copy(stages[p].at[i], landing(p, pos[a3]), 36 + p * 2 + i, a3, by)
        pick(3, 0)
        c = pltpu.make_async_copy(stages[p].at[3], landing(p, pos[a3]), local_sem.at[3 + p])
        c.start()
        local.append(c)
        fifth.append(got)
    for p in range(3):
        a3 = ORDERS[p][2]
        for i, by in enumerate((1, 3)):
            fifth[p][i].wait_recv()
            send.copy(relays[p].at[i], landing(p, lax.rem(pos[a3] + SIDE - by, SIDE), i), p * 12 + 10 + i, a3, by)
    for c in local[3:]:
        c.wait()
    for c in send.done:
        c.wait_send()
    waited = set(id(c) for group in (first, second, third, fourth, fifth) for cs in group for c in cs)
    for c in send.done:
        if id(c) not in waited:
            c.wait_recv()


def spread(wanted, mine):
    scratch = [pltpu.VMEM((4, 512, 128), BF16)]
    for make in (lambda r: (4, 4, 4, r, 128), lambda r: (4, 4, 4, 2, r, 128), lambda r: (2, 2, 4, 2, r, 128)):
        scratch += [pltpu.VMEM(make(rows), BF16) for _, rows in PIECES]
    scratch += [pltpu.SemaphoreType.DMA((42,)), pltpu.SemaphoreType.DMA((42,)), pltpu.SemaphoreType.DMA((2,)),
                pltpu.SemaphoreType.DMA((6,))]
    return pl.pallas_call(
        spread_kernel,
        in_specs=[pl.BlockSpec(memory_space=pltpu.SMEM), pl.BlockSpec(memory_space=pl.ANY)],
        out_specs=pl.BlockSpec(memory_space=pl.ANY),
        out_shape=jax.ShapeDtypeStruct((4, 4, 4, 2, 512, 128), BF16),
        scratch_shapes=scratch,
        compiler_params=pltpu.CompilerParams(collective_id=0, has_side_effects=True, vmem_limit_bytes=56 * 2**20),
        name="spread",
    )(wanted, mine)


def gather_back_kernel(wanted, back_ref, out_ref, rz0, rz1, rz2, rl0, rl1, rl2, s0, s1, s2, g0, g1, g2,
                       y0, y1, y2, yl0, yl1, yl2, h0, h1, h2, x0, x1, x2, xl0, xl1, xl2, total,
                       send_sem, recv_sem, swap_sem, local_sem):
    pos, core = place(), lax.axis_index("vintage")
    rz, rl, sums, gs = (rz0, rz1, rz2), (rl0, rl1, rl2), (s0, s1, s2), (g0, g1, g2)
    ys, yl, hs, xs, xl = (y0, y1, y2), (yl0, yl1, yl2), (h0, h1, h2), (x0, x1, x2), (xl0, xl1, xl2)
    dims = [tuple(sorted(o[:2])) for o in ORDERS]
    own = []
    send = Sender(pos, core, send_sem, recv_sem)

    def slots_of(p, level, half=None):
        a3 = ORDERS[p][2]
        r0, rows = PIECES[p]
        idx = []
        for d in range(3):
            if d == a3:
                idx.append(level)
            elif half is not None and d == dims[p][0]:
                idx.append(pl.ds(2 * half, 2))
            else:
                idx.append(slice(None))
        return back_ref.at[tuple(idx) + (slice(None), pl.ds(r0, rows), slice(None))]

    for p in range(3):
        c = pltpu.make_async_copy(slots_of(p, pos[ORDERS[p][2]]), rz[p].at[3], local_sem.at[p])
        c.start()
        own.append(c)
    greet(pos, core)

    def turn(axis, by):
        return lax.rem(pos[axis] + by, SIDE)

    zr, zd = [], []
    for p in range(3):
        a3 = ORDERS[p][2]
        zr.append([send.copy(slots_of(p, turn(a3, 2), i), rl[p].at[i], p * 18 + i, a3, by) for i, by in enumerate((1, 3))])
        zd.append([send.copy(slots_of(p, turn(a3, by)), rz[p].at[i], p * 18 + 2 + i, a3, by) for i, by in enumerate((1, 3))])
    zf = []
    for p in range(3):
        a3 = ORDERS[p][2]
        got = []
        for i, by in enumerate((1, 3)):
            zr[p][i].wait_recv()
            got.append(send.copy(rl[p].at[i], rz[p].at[2, pl.ds(2 * i, 2)], p * 18 + 4 + i, a3, by))
        zf.append(got)

    def collect(p, k, by, how):
        a3 = ORDERS[p][2]
        rows = PIECES[p][1]
        source = tile_of(shifted(pos, a3, by))

        def one(j, _):
            hi, lo = lax.div(j, SIDE), lax.rem(j, SIDE)
            holder = pos[a3] * STRIDE[a3] + hi * STRIDE[dims[p][0]] + lo * STRIDE[dims[p][1]]
            want = [wanted[source * 128 + s * 64 + holder] for s in range(2)]

            def chunk(q, _):
                at = pl.ds(pl.multiple_of(q * 16, 16), 16)
                vals = [rz[p][k, hi, lo, s, at, :].astype(F32) for s in range(2)]
                for b in range(4):
                    x = jnp.where(want[0] == b, vals[0], 0.0) + jnp.where(want[1] == b, vals[1], 0.0)
                    if how > 0:
                        x = x + sums[p][hi, lo, b, at, :]
                    if how < 2:
                        sums[p][hi, lo, b, at, :] = x
                    else:
                        gs[p][hi, lo, b, at, :] = x.astype(BF16)
                return 0
            lax.fori_loop(0, rows // 16, chunk, 0)
            return 0
        lax.fori_loop(0, SIDE * SIDE, one, 0)

    for p in range(3):
        own[p].wait()
        collect(p, 3, 0, 0)
    for i, by in enumerate((3, 1)):
        for p in range(3):
            zd[p][i].wait_recv()
            collect(p, i, by, 1)
    yr, yd = [], []

    def lines(ref, p, axis, index, half=None):
        idx = []
        for d in dims[p]:
            if d == axis:
                idx.append(index)
            else:
                idx.append(slice(None) if half is None else pl.ds(2 * half, 2))
        return ref.at[tuple(idx)]

    for p in range(3):
        a1, a2, a3 = ORDERS[p]
        for c in zf[p]:
            c.wait_recv()
        collect(p, 2, 2, 2)
        yr.append([send.copy(lines(gs[p], p, a2, turn(a2, 2), i), yl[p].at[i], p * 18 + 6 + i, a2, by) for i, by in enumerate((1, 3))])
        yd.append([send.copy(lines(gs[p], p, a2, turn(a2, by)), ys[p].at[i], p * 18 + 8 + i, a2, by) for i, by in enumerate((1, 3))])
    yf = []
    for p in range(3):
        a2 = ORDERS[p][1]
        got = []
        for i, by in enumerate((1, 3)):
            yr[p][i].wait_recv()
            got.append(send.copy(yl[p].at[i], ys[p].at[2, pl.ds(2 * i, 2)], p * 18 + 10 + i, a2, by))
        yf.append(got)
    xr, xd = [], []
    for p in range(3):
        a1, a2, a3 = ORDERS[p]
        rows = PIECES[p][1]
        for c in yd[p] + yf[p]:
            c.wait_recv()

        def add_row(j, _, p=p, a1=a1, a2=a2, rows=rows):
            i1, b = lax.div(j, 4), lax.rem(j, 4)
            mine = gs[p][tuple(i1 if d == a1 else pos[a2] for d in dims[p]) + (b,)].astype(F32)
            for k in range(3):
                mine = mine + ys[p][k, i1, b].astype(F32)
            hs[p][i1, b] = mine.astype(BF16)
            return 0
        lax.fori_loop(0, 16, add_row, 0)
        xr.append([send.copy(hs[p].at[turn(a1, 2), pl.ds(2 * i, 2)], xl[p].at[i], p * 18 + 12 + i, a1, by) for i, by in enumerate((1, 3))])
        xd.append([send.copy(hs[p].at[turn(a1, by)], xs[p].at[i], p * 18 + 14 + i, a1, by) for i, by in enumerate((1, 3))])
    xf = []
    for p in range(3):
        a1 = ORDERS[p][0]
        got = []
        for i, by in enumerate((1, 3)):
            xr[p][i].wait_recv()
            got.append(send.copy(xl[p].at[i], xs[p].at[2, pl.ds(2 * i, 2)], p * 18 + 16 + i, a1, by))
        xf.append(got)
    for p in range(3):
        a1 = ORDERS[p][0]
        r0, rows = PIECES[p]
        for c in xd[p] + xf[p]:
            c.wait_recv()
        for b in range(4):
            mine = hs[p][pos[a1], b].astype(F32)
            for k in range(3):
                mine = mine + xs[p][k, b].astype(F32)
            total[b, r0:r0 + rows, :] = mine.astype(BF16)
    swap = pltpu.make_async_remote_copy(
        src_ref=total, dst_ref=out_ref, send_sem=swap_sem.at[0], recv_sem=swap_sem.at[1],
        device_id=(1 - core, tile_of(pos)), device_id_type=MESH)
    swap.start()
    swap.wait()
    for c in send.done:
        c.wait_send()


def gather_back(wanted, back):
    scratch = []
    for make, kind in ((lambda r: (4, 4, 4, 2, r, 128), BF16), (lambda r: (2, 2, 4, 2, r, 128), BF16),
                       (lambda r: (4, 4, 4, r, 128), F32), (lambda r: (4, 4, 4, r, 128), BF16),
                       (lambda r: (3, 4, 4, r, 128), BF16), (lambda r: (2, 2, 4, r, 128), BF16),
                       (lambda r: (4, 4, r, 128), BF16),
                       (lambda r: (3, 4, r, 128), BF16), (lambda r: (2, 2, r, 128), BF16)):
        scratch += [pltpu.VMEM(make(rows), kind) for _, rows in PIECES]
    scratch += [pltpu.VMEM((4, 512, 128), BF16)]
    scratch += [pltpu.SemaphoreType.DMA((54,)), pltpu.SemaphoreType.DMA((54,)), pltpu.SemaphoreType.DMA((2,)),
                pltpu.SemaphoreType.DMA((3,))]
    return pl.pallas_call(
        gather_back_kernel,
        in_specs=[pl.BlockSpec(memory_space=pltpu.SMEM), pl.BlockSpec(memory_space=pl.ANY)],
        out_specs=pl.BlockSpec(memory_space=pl.ANY),
        out_shape=jax.ShapeDtypeStruct((4, 512, 128), BF16),
        scratch_shapes=scratch,
        compiler_params=pltpu.CompilerParams(collective_id=1, has_side_effects=True, vmem_limit_bytes=60 * 2**20),
        name="collect",
    )(wanted, back)


def shards(patches, out_grad, w_query, w_key, w_value, w_out, key_tiles, key_blocks):
    tokens, grads_in = patches[0], out_grad[0]
    my_tile = lax.axis_index("tile")
    tiles = lax.axis_size("tile")
    named = key_tiles[0].reshape(tiles, -1)
    blocks = key_blocks[0].reshape(tiles, -1)
    entries = named.shape[1]
    earlier = jnp.arange(entries)[None, :] < jnp.arange(entries)[:, None]
    rank = jnp.sum(((named[:, :, None] == named[:, None, :]) & earlier[None]).astype(jnp.int32), axis=2)
    place_of = rank * tiles + named
    hits = place_of[:, :, None] == jnp.arange(CAP * tiles, dtype=jnp.int32)[None, None, :]
    wanted = jnp.max(jnp.where(hits, blocks[:, :, None], -1), axis=1).reshape(-1)
    slots = lax.dynamic_slice_in_dim(named * CAP + rank, my_tile, 1, 0).reshape(-1)

    kv = jnp.dot(tokens, jnp.concatenate([w_key, w_value], axis=1), preferred_element_type=jnp.float32).astype(jnp.bfloat16)
    mine = kv.reshape(4, 128, 4, 128).transpose(0, 2, 1, 3).reshape(4, 512, 128)
    queries = jnp.dot(tokens, w_query, preferred_element_type=jnp.float32).astype(jnp.bfloat16)
    arrived = spread(wanted, mine)
    layer, query_grad, back = attention(slots, queries, grads_in, w_out, arrived.reshape(tiles * CAP, 512, 128), 2048, 2048)
    kv_grad = gather_back(wanted, back.reshape(4, 4, 4, CAP, 512, 128))
    kv_grad = kv_grad.reshape(4, 4, 128, 128).transpose(0, 2, 1, 3).reshape(512, 512)
    lhs = jnp.concatenate([query_grad, kv_grad], axis=1)
    rhs = jnp.concatenate([w_query, w_key, w_value], axis=1)
    total = lax.dot_general(lhs, rhs, (((1,), (1,)), ((), ())), preferred_element_type=jnp.float32)
    return layer[None], total.astype(jnp.bfloat16)[None]


def solution(mesh):
    cubes = P("vintage", "tile", None)
    lists = P("vintage", None, None)
    return jax.shard_map(shards, mesh=mesh, in_specs=(cubes, cubes, P(), P(), P(), P(), lists, lists),
                         out_specs=(cubes, cubes), check_vma=False)
```

time: 1130 us -> 313 us (0.28)
  the two profiles are of different devices: /device:TPU:127 before, /device:TPU:1 now
where the time goes in v1:
time: 313 us; the launch traced here: 312 us
  Pallas kernels  297 us (95%)
  matrix products  5.59 us (2%)
  local copies, waits for them, and re-layouts  4.79 us (2%)
  other arithmetic  4.49 us (1%)
    pallas_call x1, Pallas kernels, gather_back(): pl.pallas_call(gather_back_kernel, in_specs=[pl.BlockSpec(memory_space=pl...  122 us
    pallas_call x1, Pallas kernels, spread(): pl.pallas_call(spread_kernel, in_specs=[pl.BlockSpec(memory_space=pltpu.S...  109 us
    pallas_call x1, Pallas kernels, attention(): pl.pallas_call(functools.partial(attend_kernel, NC1=NC1, NC2=NC2), grid_s...  65.4 us

profile of v1, /device:TPU:1, one launch (start us, length us, event | category | flops | bytes accessed | tf_op | source)
XLA Modules:
  0.0 312.2 jit_solution(3363471918445619283)
XLA Ops:
  0.6 0.0 copy-start
  0.7 0.9 copy.16
  1.6 0.1 reshape_squeeze.3
  1.6 1.9 convert_reduce_fusion
  3.5 0.6 fusion.23.slots
  4.1 0.8 copy.17
  4.9 0.1 broadcast_in_dim.25
  5.0 2.0 select_reduce_fusion
  7.0 0.0 copy-done
  7.1 1.8 fusion.17
  8.9 0.1 reshape.53
  9.0 1.1 copy.18
  10.1 0.0 copy-done.1
  10.1 1.7 convolution_convert_fusion.q_ref
  11.8 108.9 %spread.1 = bf16[4,4,4,2,512,128]{5,4,3,2,1,0:T(8,128)(2,1)} custom-call(s32[8192]{0:T(1024)} %bitcast.37, bf16[4,512,128]{2,1,0:T(8,128)(2,1)} %bitcast.32), custom_call_target="tpu_custom_call" | custom-call | tf_op jit(solution)/shard_map/spread/pallas_call | solution.py:381
  120.7 65.4 %attend.1 = (bf16[512,768]{1,0:T(8,128)(2,1)}, bf16[512,768]{1,0:T(8,128)(2,1)}, bf16[128,512,128]{2,1,0:T(8,128)(2,1)}) custom-call(s32[64]{0:T(128)} %fusion.23.slots, bf16[512,768]{1,0:T(8,128)(2,1)} %convolution_convert_fusion.q_ref, bf16[512,768]{1,0:T(8,128)(2,1)} %bitcast.35, bf16[768,768]{1,0:T(8,128)(2,1)} %wo_ref.1, bf16[128,512,128]{2,1,0:T(8,128)(2,1)} %bitcast.30), custom_call_target="tpu_custom_call" | custom-call | tf_op jit(solution)/shard_map/attend/pallas_call | solution.py:186
  186.1 122.3 %collect.1 = bf16[4,512,128]{2,1,0:T(8,128)(2,1)} custom-call(s32[8192]{0:T(1024)} %bitcast.38, bf16[4,4,4,2,512,128]{5,4,3,2,1,0:T(8,128)(2,1)} %bitcast.31), custom_call_target="tpu_custom_call" | custom-call | tf_op jit(solution)/shard_map/collect/pallas_call | solution.py:552
  308.4 0.0 copy-start.2
  308.4 0.0 copy-start.3
  308.4 0.0 copy-start.4
  308.4 1.6 copy.19
  310.0 0.1 copy.22
  310.1 0.0 copy-done.2
  310.1 2.1 fusion.12
  (5 shorter events, 0.0 us)
Async XLA Ops:
  0.6 6.4 %copy-start = (bf16[1,512,768]{2,1,0:T(8,128)(2,1)S(1)}, bf16[1,512,768]{2,1,0:T(8,128)(2,1)}, u32[]{:S(2)}) copy-start(bf16[1,512,768]{2,1,0:T(8,128)(2,1)} %param.8) | copy-start | bytes 2359300
  7.1 3.1 copy-start.1
  308.4 1.7 copy-start.2
  308.4 1.7 copy-start.3
  308.4 1.7 copy-start.4

commit v2 on v1

v2 whole, which is shorter than its diff:
```python
import functools

import jax
import jax.numpy as jnp
from jax import lax
from jax.experimental import pallas as pl
from jax.experimental.pallas import tpu as pltpu
from jax.sharding import PartitionSpec as P

CAP = 2
LOG2E = 1.4426950408889634
EPSILON = 1e-06
F32, BF16 = jnp.float32, jnp.bfloat16


def dot(a, b, ca=1, cb=0):
    return lax.dot_general(a, b, (((ca,), (cb,)), ((), ())), preferred_element_type=F32)


def attend_kernel(slots, q_ref, go_ref, wo_ref, arr_ref, lay_ref, qp_ref, dop_ref, stat_ref, inv_ref, ent_ref,
                  kv, e, acc, att, in_sem, out_sem):
    b, nb = pl.program_id(0), pl.num_programs(0)
    L = kv.shape[1]
    cur = lax.rem(b, 2)

    def fetch(blk, slot):
        return [pltpu.make_async_copy(arr_ref.at[slots[blk * L + l]], kv.at[slot, l], in_sem.at[slot, l]) for l in range(L)]

    def keep(blk, slot):
        return [pltpu.make_async_copy(kv.at[slot, :, g], ent_ref.at[g, pl.ds(blk * L, L)], out_sem.at[slot, g]) for g in range(4)]

    @pl.when(b == 0)
    def _():
        for c in fetch(0, 0):
            c.start()

    @pl.when(b >= 1)
    def _():
        for c in keep(b - 1, 1 - cur):
            c.wait()

    @pl.when(b + 1 < nb)
    def _():
        for c in fetch(b + 1, 1 - cur):
            c.start()

    @pl.when(b == 0)
    def _():
        def clear(i, _):
            inv_ref[i] = 0
            return 0
        lax.fori_loop(0, inv_ref.shape[0], clear, 0)

        def put(i, _):
            inv_ref[slots[i]] = i
            return 0
        lax.fori_loop(0, nb * L, put, 0)

    zero = jnp.zeros((128, 64), BF16)
    for h in range(12):
        x = q_ref[:, (h // 2) * 128:(h // 2) * 128 + 128][:, (h % 2) * 64:(h % 2) * 64 + 64]
        qp_ref[h // 3, (h % 3) * 128:(h % 3) * 128 + 128, :] = jnp.concatenate([x, zero], axis=1)
    for c in fetch(b, cur):
        c.wait()
    for c in keep(b, cur):
        c.start()

    for g in range(4):
        m, inv, out = attend_rows(qp_ref[g], kv[cur, :, g].reshape(L * 128, 128), e)
        stat_ref[g] = jnp.concatenate([m[:, :64], inv[:, 64:]], axis=1)
        acc[g] = out

    ss = jnp.zeros((128, 128), F32)
    for j in range(6):
        a = jnp.concatenate([acc[h // 3, (h % 3) * 128:(h % 3) * 128 + 128, :][:, 64:] for h in (2 * j, 2 * j + 1)], axis=1)
        a = a.astype(BF16).astype(F32)
        att[:, j * 128:j * 128 + 128] = a
        ss = ss + a * a
    root = jnp.sqrt(jnp.sum(ss, axis=1, keepdims=True) * (1.0 / 768) + EPSILON)
    normed = att[...] / root
    lay_ref[...] = dot(normed.astype(BF16), wo_ref[...]).astype(BF16)
    ng = dot(go_ref[...], wo_ref[...], 1, 1)
    att[...] = (ng - normed * (jnp.sum(ng * normed, axis=1, keepdims=True) * (1.0 / 768))) / root
    for h in range(12):
        x = att[:, (h // 2) * 128:(h // 2) * 128 + 128][:, (h % 2) * 64:(h % 2) * 64 + 64].astype(BF16)
        dop_ref[h // 3, (h % 3) * 128:(h % 3) * 128 + 128, :] = jnp.concatenate([zero, x], axis=1)

    @pl.when(b == nb - 1)
    def _():
        for c in keep(b, cur):
            c.wait()


SCALE = 0.125 * LOG2E


def attend_rows(q, kv, e):
    rows, n = q.shape[0], kv.shape[0] // 128
    s = dot(q, kv, 1, 1)
    m = s[:, :128]
    for i in range(1, n):
        m = jnp.maximum(m, s[:, i * 128:i * 128 + 128])
    m = jnp.broadcast_to(jnp.max(m, axis=1, keepdims=True), (rows, 128))
    total = jnp.zeros((rows, 128), F32)
    for i in range(n):
        x = jnp.exp2((s[:, i * 128:i * 128 + 128] - m) * SCALE)
        e[:, i * 128:i * 128 + 128] = x
        total = total + x
    inv = jnp.broadcast_to(1.0 / jnp.sum(total, axis=1, keepdims=True), (rows, 128))
    low = jnp.concatenate([(e[:, i * 128:i * 128 + 128] * inv).astype(BF16) for i in range(n)], axis=1)
    return m, inv, dot(low, kv)


def attention(slots, queries, grads, w_out, arr):
    rows, D = queries.shape
    nb = rows // 128
    L = slots.shape[0] // nb
    ns = arr.shape[0]
    row = lambda b, s: (b, 0)
    padded = lambda b, s: (b, 0, 0, 0)
    return pl.pallas_call(
        attend_kernel,
        grid_spec=pltpu.PrefetchScalarGridSpec(
            num_scalar_prefetch=1, grid=(nb,),
            in_specs=[pl.BlockSpec((128, D), row), pl.BlockSpec((128, D), row),
                      pl.BlockSpec((D, D), lambda b, s: (0, 0), pipeline_mode=pl.Buffered(1)),
                      pl.BlockSpec(memory_space=pl.ANY)],
            out_specs=[pl.BlockSpec((128, D), row)] + [pl.BlockSpec((None, 4, 384, 128), padded)] * 3
                      + [pl.BlockSpec(memory_space=pltpu.SMEM), pl.BlockSpec(memory_space=pl.ANY)],
            scratch_shapes=[
                pltpu.VMEM((2, L, 4, 128, 128), BF16), pltpu.VMEM((384, 2048), F32),
                pltpu.VMEM((4, 384, 128), F32), pltpu.VMEM((128, 768), F32),
                pltpu.SemaphoreType.DMA((2, L)), pltpu.SemaphoreType.DMA((2, 4))]),
        out_shape=[jax.ShapeDtypeStruct((rows, D), BF16), jax.ShapeDtypeStruct((nb, 4, 384, 128), BF16),
                   jax.ShapeDtypeStruct((nb, 4, 384, 128), BF16), jax.ShapeDtypeStruct((nb, 4, 384, 128), F32),
                   jax.ShapeDtypeStruct((ns,), jnp.int32), jax.ShapeDtypeStruct((4, nb * L, 128, 128), BF16)],
        compiler_params=pltpu.CompilerParams(dimension_semantics=("arbitrary",), vmem_limit_bytes=60 * 2**20),
        name="attend",
    )(slots, queries, grads, w_out, arr.reshape(ns, 4, 128, 128))


MESH = pl.DeviceIdType.MESH
SIDE = 4
ORDERS = ((0, 1, 2), (1, 2, 0), (2, 0, 1))
PIECES = ((0, 176), (176, 176), (352, 160))
STRIDE = (16, 4, 1)


def place():
    tile = lax.axis_index("tile")
    return [lax.rem(lax.div(tile, s), SIDE) for s in STRIDE]


def shifted(pos, axis, by):
    moved = list(pos)
    moved[axis] = lax.rem(pos[axis] + by, SIDE)
    return moved


def tile_of(pos):
    return pos[0] * 16 + pos[1] * 4 + pos[2]


def greet(pos, core, wait=True):
    barrier = pltpu.get_barrier_semaphore()
    for axis in range(3):
        for by in (1, 3):
            pl.semaphore_signal(barrier, inc=1, device_id=(core, tile_of(shifted(pos, axis, by))), device_id_type=MESH)
    pl.semaphore_signal(barrier, inc=1, device_id=(1 - core, tile_of(pos)), device_id_type=MESH)
    if wait:
        greet_wait()


def greet_wait():
    pl.semaphore_wait(pltpu.get_barrier_semaphore(), 7)


class Sender:
    def __init__(self, pos, core, send_sem, recv_sem):
        self.pos, self.core, self.send_sem, self.recv_sem = pos, core, send_sem, recv_sem
        self.done = []

    def copy(self, src, dst, sem, axis, by):
        c = pltpu.make_async_remote_copy(
            src_ref=src, dst_ref=dst, send_sem=self.send_sem.at[sem], recv_sem=self.recv_sem.at[sem],
            device_id=(self.core, tile_of(shifted(self.pos, axis, by))), device_id_type=MESH)
        c.start()
        self.done.append(c)
        return c


def at_axis(ref, dims, index, axis, *rest):
    return ref.at[tuple(index if d == axis else slice(None) for d in dims) + rest]


def spread_kernel(wanted, mine_ref, out_ref, own, plane0, plane1, plane2, st0, st1, st2, rl0, rl1, rl2,
                  send_sem, recv_sem, swap_sem, local_sem):
    pos, core = place(), lax.axis_index("vintage")
    planes, stages, relays = (plane0, plane1, plane2), (st0, st1, st2), (rl0, rl1, rl2)
    greet(pos, core)
    swap = pltpu.make_async_remote_copy(
        src_ref=mine_ref, dst_ref=own, send_sem=swap_sem.at[0], recv_sem=swap_sem.at[1],
        device_id=(1 - core, tile_of(pos)), device_id_type=MESH)
    swap.start()
    swap.wait()
    send = Sender(pos, core, send_sem, recv_sem)
    dims = [tuple(sorted(o[:2])) for o in ORDERS]
    local = []

    def line(p, axis):
        return at_axis(planes[p], dims[p], pos[axis], axis)

    def cell(p, a1, i1, a2, i2, *rest):
        return planes[p].at[tuple(i1 if d == a1 else i2 for d in dims[p]) + rest]

    for p, (r0, rows) in enumerate(PIECES):
        a1, a2, a3 = ORDERS[p]
        c = pltpu.make_async_copy(own.at[:, pl.ds(r0, rows), :], cell(p, a1, pos[a1], a2, pos[a2]), local_sem.at[p])
        c.start()
        local.append(c)
    first = []
    for p in range(3):
        a1, a2, a3 = ORDERS[p]
        local[p].wait()
        here = cell(p, a1, pos[a1], a2, pos[a2])
        first.append([send.copy(here, here, p * 12 + i, a1, by) for i, by in enumerate((1, 3))])
    second = []
    for p in range(3):
        a1, a2, a3 = ORDERS[p]
        got = []
        for i, by in enumerate((1, 3)):
            first[p][i].wait_recv()
            part = cell(p, a1, lax.rem(pos[a1] + SIDE - by, SIDE), a2, pos[a2], pl.ds(2 * i, 2))
            got.append(send.copy(part, part, p * 12 + 2 + i, a1, by))
        second.append(got)
    third = []
    for p in range(3):
        a1, a2, a3 = ORDERS[p]
        for c in second[p]:
            c.wait_recv()
        here = line(p, a2)
        third.append([send.copy(here, here, p * 12 + 4 + i, a2, by) for i, by in enumerate((1, 3))])
    fourth = []
    for p in range(3):
        a1, a2, a3 = ORDERS[p]
        got = []
        for i, by in enumerate((1, 3)):
            third[p][i].wait_recv()
            other = lax.rem(pos[a2] + SIDE - by, SIDE)
            part = planes[p].at[tuple(other if d == a2 else pl.ds(2 * i, 2) for d in dims[p])]
            got.append(send.copy(part, part, p * 12 + 6 + i, a2, by))
        fourth.append(got)

    def landing(p, source, half=None):
        a3 = ORDERS[p][2]
        r0, rows = PIECES[p]
        idx = []
        for d in range(3):
            if d == a3:
                idx.append(source)
            elif half is not None and d == dims[p][0]:
                idx.append(pl.ds(2 * half, 2))
            else:
                idx.append(slice(None))
        return out_ref.at[tuple(idx) + (slice(None), pl.ds(r0, rows), slice(None))]

    fifth = []
    for p in range(3):
        a1, a2, a3 = ORDERS[p]
        r0, rows = PIECES[p]
        for c in fourth[p]:
            c.wait_recv()

        def pick(k, by, p=p, a3=a3):
            dest = tile_of(shifted(pos, a3, by))

            def one(j, _):
                hi, lo = lax.div(j, SIDE), lax.rem(j, SIDE)
                source = pos[a3] * STRIDE[a3] + hi * STRIDE[dims[p][0]] + lo * STRIDE[dims[p][1]]
                for s in range(2):
                    blk = jnp.maximum(wanted[dest * 128 + s * 64 + source], 0)
                    stages[p][k, hi, lo, s] = planes[p][hi, lo, blk]
                return 0
            lax.fori_loop(0, SIDE * SIDE, one, 0)

        got = []
        pick(2, 2)
        for i, by in enumerate((1, 3)):
            got.append(send.copy(stages[p].at[2, pl.ds(2 * i, 2)], relays[p].at[i], p * 12 + 8 + i, a3, by))
        for i, by in enumerate((1, 3)):
            pick(i, by)
            send.copy(stages[p].at[i], landing(p, pos[a3]), 36 + p * 2 + i, a3, by)
        pick(3, 0)
        c = pltpu.make_async_copy(stages[p].at[3], landing(p, pos[a3]), local_sem.at[3 + p])
        c.start()
        local.append(c)
        fifth.append(got)
    for p in range(3):
        a3 = ORDERS[p][2]
        for i, by in enumerate((1, 3)):
            fifth[p][i].wait_recv()
            send.copy(relays[p].at[i], landing(p, lax.rem(pos[a3] + SIDE - by, SIDE), i), p * 12 + 10 + i, a3, by)
    for c in local[3:]:
        c.wait()
    for c in send.done:
        c.wait_send()
    waited = set(id(c) for group in (first, second, third, fourth, fifth) for cs in group for c in cs)
    for c in send.done:
        if id(c) not in waited:
            c.wait_recv()


def spread(wanted, mine):
    scratch = [pltpu.VMEM((4, 512, 128), BF16)]
    for make in (lambda r: (4, 4, 4, r, 128), lambda r: (4, 4, 4, 2, r, 128), lambda r: (2, 2, 4, 2, r, 128)):
        scratch += [pltpu.VMEM(make(rows), BF16) for _, rows in PIECES]
    scratch += [pltpu.SemaphoreType.DMA((42,)), pltpu.SemaphoreType.DMA((42,)), pltpu.SemaphoreType.DMA((2,)),
                pltpu.SemaphoreType.DMA((6,))]
    return pl.pallas_call(
        spread_kernel,
        in_specs=[pl.BlockSpec(memory_space=pltpu.SMEM), pl.BlockSpec(memory_space=pl.ANY)],
        out_specs=pl.BlockSpec(memory_space=pl.ANY),
        out_shape=jax.ShapeDtypeStruct((4, 4, 4, 2, 512, 128), BF16),
        scratch_shapes=scratch,
        compiler_params=pltpu.CompilerParams(collective_id=0, has_side_effects=True, vmem_limit_bytes=56 * 2**20),
        name="spread",
    )(wanted, mine)


CUTS = ((48, 48, 32), (48, 32, 48), (32, 48, 48), (48, 48, 32))


def spans(g):
    start = 0
    out = []
    for rows in CUTS[g]:
        out.append((start, rows))
        start += rows
    return out


def return_kernel(wanted, inv, qp_ref, dop_ref, stat_ref, ent_ref, dq_ref, out_ref, rl_ref, yl_ref, xl_ref,
                  kvb, p, t, dqs, parts, stage, rz, sums, gs, ys, hs, xs, total,
                  send_sem, recv_sem, swap_sem, kv_sem):
    pos, core = place(), lax.axis_index("vintage")
    dims = [tuple(sorted(o[:2])) for o in ORDERS]
    send = Sender(pos, core, send_sem, recv_sem)
    nb = qp_ref.shape[0]
    L = kvb.shape[1]
    greet(pos, core, False)

    def turn(axis, by):
        return lax.rem(pos[axis] + by, SIDE)

    def key(g, p, i):
        return (g * 3 + p) * 18 + i

    def load(g, b, slot):
        return pltpu.make_async_copy(ent_ref.at[g, pl.ds(b * L, L)], kvb.at[slot], kv_sem.at[slot])

    load(0, 0, 0).start()

    def backward(g):
        def one(b, _):
            cur = lax.rem(b, 2)
            load(g, b, cur).wait()

            @pl.when(b + 1 < nb)
            def _():
                load(g, b + 1, 1 - cur).start()

            if g < 3:
                @pl.when(b + 1 == nb)
                def _():
                    load(g + 1, 0, 0).start()

            kv = kvb[cur].reshape(L * 128, 128)
            q, do = qp_ref[b, g], dop_ref[b, g]
            m = jnp.broadcast_to(stat_ref[b, g, :, 0:1], (384, 128))
            nrm = jnp.broadcast_to(stat_ref[b, g, :, 64:65], (384, 128))
            s = dot(q, kv, 1, 1)
            dp = dot((do.astype(F32) * 0.125).astype(BF16), kv, 1, 1)
            rd = jnp.zeros((384, 128), F32)
            for i in range(L):
                cols = slice(i * 128, i * 128 + 128)
                pr = jnp.exp2((s[:, cols] - m) * SCALE) * nrm
                x = pr * dp[:, cols]
                p[:, cols] = pr
                t[:, cols] = x
                rd = rd + x
            rd = jnp.broadcast_to(jnp.sum(rd, axis=1, keepdims=True), (384, 128))
            ds_, low = [], []
            for i in range(L):
                cols = slice(i * 128, i * 128 + 128)
                pr = p[:, cols]
                ds_.append((t[:, cols] - pr * rd).astype(BF16))
                low.append(pr.astype(BF16))
            ds_, low = jnp.concatenate(ds_, axis=1), jnp.concatenate(low, axis=1)
            dqs[b, g] = dot(ds_, kv).astype(BF16)
            part = dot(jnp.concatenate([ds_, low], axis=0), jnp.concatenate([q, do], axis=0), 0, 0)
            parts[pl.ds(b * L, L)] = part.astype(BF16).reshape(L, 128, 128)
            return 0
        lax.fori_loop(0, nb, one, 0)

    zr, zd, zf, yr, yd, yf, xr, xd, xf = [{} for _ in range(9)]

    def slots_of(g, p, level, half=None):
        a3 = ORDERS[p][2]
        r0, rows = spans(g)[p]
        idx = []
        for d in range(3):
            if d == a3:
                idx.append(level)
            elif half is not None and d == dims[p][0]:
                idx.append(pl.ds(2 * half, 2))
            else:
                idx.append(slice(None))
        return stage.at[(g % 2,) + tuple(idx) + (slice(None), pl.ds(r0, rows), slice(None))]

    def at_rows(ref, g, p, lead):
        r0, rows = spans(g)[p]
        return ref.at[(g,) + tuple(lead) + (pl.ds(r0, rows), slice(None))]

    W = slice(None)

    def z_send(g):
        if g >= 2:
            for c in zr[g - 2] + zd[g - 2]:
                c.wait_send()

        def place_part(j, _):
            x, y, z = lax.div(j, 16), lax.rem(lax.div(j, 4), 4), lax.rem(j, 4)
            for s in range(2):
                stage[g % 2, x, y, z, s] = parts[inv[j * 2 + s]]
            return 0
        lax.fori_loop(0, 64, place_part, 0)
        if g == 0:
            greet_wait()
        zr[g], zd[g] = [], []
        for p in range(3):
            a3 = ORDERS[p][2]
            for i, by in enumerate((1, 3)):
                zr[g].append(send.copy(slots_of(g, p, turn(a3, 2), i), at_rows(rl_ref, g, p, (i, W, W, W)), key(g, p, i), a3, by))
        for p in range(3):
            a3 = ORDERS[p][2]
            for i, by in enumerate((1, 3)):
                zd[g].append(send.copy(slots_of(g, p, turn(a3, by)), at_rows(rz, g, p, (i, W, W, W)), key(g, p, 2 + i), a3, by))

    def z_relay(g):
        zf[g] = []
        for p in range(3):
            a3 = ORDERS[p][2]
            for i, by in enumerate((1, 3)):
                zr[g][p * 2 + i].wait_recv()
                zf[g].append(send.copy(at_rows(rl_ref, g, p, (i, W, W, W)), at_rows(rz, g, p, (2, pl.ds(2 * i, 2), W, W)),
                                       key(g, p, 4 + i), a3, by))

    def add_up(g, p, k, by, first, last):
        a3 = ORDERS[p][2]
        r0, rows = spans(g)[p]
        source = tile_of(shifted(pos, a3, by))

        def one(j, _):
            hi, lo = lax.div(j, SIDE), lax.rem(j, SIDE)
            holder = pos[a3] * STRIDE[a3] + hi * STRIDE[dims[p][0]] + lo * STRIDE[dims[p][1]]
            where = [None] * 3
            where[a3], where[dims[p][0]], where[dims[p][1]] = pos[a3], hi, lo
            vals = []
            for s in range(2):
                at = (k, hi, lo, s) if k < 3 else tuple(where) + (s,)
                ref, lead = (rz, g) if k < 3 else (stage, g % 2)
                vals.append(ref[(lead,) + at + (pl.ds(r0, rows), slice(None))].astype(F32))
            want = [wanted[source * 128 + s * 64 + holder] for s in range(2)]
            for b in range(4):
                x = jnp.where(want[0] == b, vals[0], 0.0) + jnp.where(want[1] == b, vals[1], 0.0)
                if not first:
                    x = x + sums[hi, lo, b, pl.ds(r0, rows), :]
                if last:
                    gs[g, hi, lo, b, pl.ds(r0, rows), :] = x.astype(BF16)
                else:
                    sums[hi, lo, b, pl.ds(r0, rows), :] = x
            return 0
        lax.fori_loop(0, SIDE * SIDE, one, 0)

    def z_sum(g):
        for p in range(3):
            add_up(g, p, 3, 0, True, False)
        for i, by in enumerate((3, 1)):
            for p in range(3):
                zd[g][p * 2 + i].wait_recv()
                add_up(g, p, i, by, False, False)

    def lines(g, p, axis, index, half=None):
        idx = []
        for d in dims[p]:
            if d == axis:
                idx.append(index)
            else:
                idx.append(slice(None) if half is None else pl.ds(2 * half, 2))
        return at_rows(gs, g, p, tuple(idx) + (W,))

    def y_send(g):
        yr[g], yd[g] = [], []
        for p in range(3):
            a2 = ORDERS[p][1]
            for c in zf[g][p * 2:p * 2 + 2]:
                c.wait_recv()
            add_up(g, p, 2, 2, False, True)
        for p in range(3):
            a2 = ORDERS[p][1]
            for i, by in enumerate((1, 3)):
                yr[g].append(send.copy(lines(g, p, a2, turn(a2, 2), i), at_rows(yl_ref, g, p, (i, W, W)), key(g, p, 6 + i), a2, by))
        for p in range(3):
            a2 = ORDERS[p][1]
            for i, by in enumerate((1, 3)):
                yd[g].append(send.copy(lines(g, p, a2, turn(a2, by)), at_rows(ys, g, p, (i, W, W)), key(g, p, 8 + i), a2, by))

    def y_relay(g):
        yf[g] = []
        for p in range(3):
            a2 = ORDERS[p][1]
            for i, by in enumerate((1, 3)):
                yr[g][p * 2 + i].wait_recv()
                yf[g].append(send.copy(at_rows(yl_ref, g, p, (i, W, W)), at_rows(ys, g, p, (2, pl.ds(2 * i, 2), W)),
                                       key(g, p, 10 + i), a2, by))

    def x_send(g):
        xr[g], xd[g] = [], []
        for p in range(3):
            a1, a2, a3 = ORDERS[p]
            r0, rows = spans(g)[p]
            at = (pl.ds(r0, rows), slice(None))
            for c in yd[g][p * 2:p * 2 + 2] + yf[g][p * 2:p * 2 + 2]:
                c.wait_recv()

            def row(j, _, p=p, a1=a1, a2=a2, at=at):
                i1, b = lax.div(j, 4), lax.rem(j, 4)
                mine = gs[(g,) + tuple(i1 if d == a1 else pos[a2] for d in dims[p]) + (b,) + at].astype(F32)
                for k in range(3):
                    mine = mine + ys[(g, k, i1, b) + at].astype(F32)
                hs[(g, i1, b) + at] = mine.astype(BF16)
                return 0
            lax.fori_loop(0, 16, row, 0)
        for p in range(3):
            a1 = ORDERS[p][0]
            for i, by in enumerate((1, 3)):
                xr[g].append(send.copy(at_rows(hs, g, p, (turn(a1, 2), pl.ds(2 * i, 2))), at_rows(xl_ref, g, p, (i, W)), key(g, p, 12 + i), a1, by))
        for p in range(3):
            a1 = ORDERS[p][0]
            for i, by in enumerate((1, 3)):
                xd[g].append(send.copy(at_rows(hs, g, p, (turn(a1, by), W)), at_rows(xs, g, p, (i, W)), key(g, p, 14 + i), a1, by))

    def x_relay(g):
        xf[g] = []
        for p in range(3):
            a1 = ORDERS[p][0]
            for i, by in enumerate((1, 3)):
                xr[g][p * 2 + i].wait_recv()
                xf[g].append(send.copy(at_rows(xl_ref, g, p, (i, W)), at_rows(xs, g, p, (2, pl.ds(2 * i, 2))),
                                       key(g, p, 16 + i), a1, by))

    swaps = []

    def finish(g):
        for p in range(3):
            a1 = ORDERS[p][0]
            r0, rows = spans(g)[p]
            at = (pl.ds(r0, rows), slice(None))
            for c in xd[g][p * 2:p * 2 + 2] + xf[g][p * 2:p * 2 + 2]:
                c.wait_recv()
            for b in range(4):
                mine = hs[(g, pos[a1], b) + at].astype(F32)
                for k in range(3):
                    mine = mine + xs[(g, k, b) + at].astype(F32)
                total[(g, b) + at] = mine.astype(BF16)
        c = pltpu.make_async_remote_copy(
            src_ref=total.at[g], dst_ref=out_ref.at[g], send_sem=swap_sem.at[0, g], recv_sem=swap_sem.at[1, g],
            device_id=(1 - core, tile_of(pos)), device_id_type=MESH)
        c.start()
        swaps.append(c)

    def queries_out(b):
        for j in range(6):
            dq_ref[b * 128:b * 128 + 128, j * 128:j * 128 + 128] = jnp.concatenate(
                [dqs[b, h // 3, (h % 3) * 128:(h % 3) * 128 + 128, :][:, :64] for h in (2 * j, 2 * j + 1)], axis=1)

    backward(0)
    z_send(0)
    backward(1)
    z_send(1)
    z_relay(0)
    z_sum(0)
    backward(2)
    z_send(2)
    z_relay(1)
    y_send(0)
    z_sum(1)
    backward(3)
    z_send(3)
    z_relay(2)
    y_send(1)
    y_relay(0)
    z_sum(2)
    z_relay(3)
    y_send(2)
    y_relay(1)
    x_send(0)
    z_sum(3)
    y_send(3)
    y_relay(2)
    x_send(1)
    x_relay(0)
    for b in range(4):
        queries_out(b)
    y_relay(3)
    x_send(2)
    x_relay(1)
    finish(0)
    x_send(3)
    x_relay(2)
    finish(1)
    x_relay(3)
    finish(2)
    finish(3)
    for c in swaps:
        c.wait()
    for g in range(4):
        late = zr[g] + zd[g] if g >= 2 else []
        for c in late + zf[g] + yr[g] + yd[g] + yf[g] + xr[g] + xd[g] + xf[g]:
            c.wait_send()


def gather_back(wanted, inv, qp, dop, stat, ent):
    V, A = pl.BlockSpec(memory_space=pltpu.VMEM), pl.BlockSpec(memory_space=pl.ANY)
    S = pl.BlockSpec(memory_space=pltpu.SMEM)
    bf = lambda *shape: jax.ShapeDtypeStruct(shape, BF16)
    vm = lambda *shape: pltpu.VMEM(shape, BF16)
    out = pl.pallas_call(
        return_kernel,
        in_specs=[S, S, V, V, V, A],
        out_specs=[V, A, A, A, A],
        out_shape=[bf(512, 768), bf(4, 4, 128, 128), bf(4, 2, 2, 4, 2, 128, 128), bf(4, 2, 2, 4, 128, 128), bf(4, 2, 2, 128, 128)],
        scratch_shapes=[
            vm(2, 16, 128, 128), pltpu.VMEM((384, 2048), F32), pltpu.VMEM((384, 2048), F32), vm(4, 4, 384, 128),
            vm(64, 128, 128), vm(2, 4, 4, 4, 2, 128, 128), vm(4, 3, 4, 4, 2, 128, 128),
            pltpu.VMEM((4, 4, 4, 128, 128), F32), vm(4, 4, 4, 4, 128, 128), vm(4, 3, 4, 4, 128, 128),
            vm(4, 4, 4, 128, 128), vm(4, 3, 4, 128, 128), vm(4, 4, 128, 128),
            pltpu.SemaphoreType.DMA((216,)), pltpu.SemaphoreType.DMA((216,)), pltpu.SemaphoreType.DMA((2, 4)),
            pltpu.SemaphoreType.DMA((2,))],
        compiler_params=pltpu.CompilerParams(collective_id=1, has_side_effects=True, vmem_limit_bytes=67043328),
        name="collect",
    )(wanted, inv, qp, dop, stat, ent)
    return out[0], out[1]


def shards(patches, out_grad, w_query, w_key, w_value, w_out, key_tiles, key_blocks):
    tokens, grads_in = patches[0], out_grad[0]
    my_tile = lax.axis_index("tile")
    tiles = lax.axis_size("tile")
    named = key_tiles[0].reshape(tiles, -1)
    blocks = key_blocks[0].reshape(tiles, -1)
    entries = named.shape[1]
    earlier = jnp.arange(entries)[None, :] < jnp.arange(entries)[:, None]
    rank = jnp.sum(((named[:, :, None] == named[:, None, :]) & earlier[None]).astype(jnp.int32), axis=2)
    place_of = rank * tiles + named
    hits = place_of[:, :, None] == jnp.arange(CAP * tiles, dtype=jnp.int32)[None, None, :]
    wanted = jnp.max(jnp.where(hits, blocks[:, :, None], -1), axis=1).reshape(-1)
    slots = lax.dynamic_slice_in_dim(named * CAP + rank, my_tile, 1, 0).reshape(-1)

    w_kv = jnp.concatenate([w_key.reshape(-1, 4, 64), w_value.reshape(-1, 4, 64)], axis=2).reshape(-1, 512)
    kv = jnp.dot(tokens, w_kv, preferred_element_type=jnp.float32).astype(jnp.bfloat16)
    mine = kv.reshape(4, 128, 4, 128).transpose(0, 2, 1, 3).reshape(4, 512, 128)
    queries = jnp.dot(tokens, w_query, preferred_element_type=jnp.float32).astype(jnp.bfloat16)
    arrived = spread(wanted, mine)
    layer, qp, dop, stat, inv, ent = attention(slots, queries, grads_in, w_out, arrived.reshape(tiles * CAP, 512, 128))
    query_grad, kv_grad = gather_back(wanted, inv, qp, dop, stat, ent)
    kv_grad = kv_grad.transpose(1, 2, 0, 3).reshape(512, 512)
    lhs = jnp.concatenate([query_grad, kv_grad], axis=1)
    rhs = jnp.concatenate([w_query, w_kv], axis=1)
    total = lax.dot_general(lhs, rhs, (((1,), (1,)), ((), ())), preferred_element_type=jnp.float32)
    return layer[None], total.astype(jnp.bfloat16)[None]


def solution(mesh):
    cubes = P("vintage", "tile", None)
    lists = P("vintage", None, None)
    return jax.shard_map(shards, mesh=mesh, in_specs=(cubes, cubes, P(), P(), P(), P(), lists, lists),
                         out_specs=(cubes, cubes), check_vma=False)
```

time: 313 us -> 292 us (0.933)
  Pallas kernels: 297 us -> 273 us
    pallas_call x2, Pallas kernels: 188 us -> 164 us  [the longest x1 132 us: gather_back(): pl.pallas_call(return_kernel, in_specs=[S, S, V, V, V, A], out_specs=[V,...]
where the time goes in v2:
time: 292 us; the launch traced here: 291 us
  Pallas kernels  273 us (93%)
  local copies, waits for them, and re-layouts  7.29 us (2%)
  matrix products  5.49 us (2%)
  other arithmetic  4.49 us (2%)
    pallas_call x1, Pallas kernels, gather_back(): pl.pallas_call(return_kernel, in_specs=[S, S, V, V, V, A], out_specs=[V,...  132 us
    pallas_call x1, Pallas kernels, spread(): pl.pallas_call(spread_kernel, in_specs=[pl.BlockSpec(memory_space=pltpu.S...  109 us
    pallas_call x1, Pallas kernels, attention(): pl.pallas_call(attend_kernel, grid_spec=pltpu.PrefetchScalarGridSpec(num_...  32.5 us

profile of v2, /device:TPU:1, one launch (start us, length us, event | category | flops | bytes accessed | tf_op | source)
XLA Modules:
  0.0 291.3 jit_solution(12826439827669293573)
XLA Ops:
  0.6 0.0 copy-start.1
  0.7 0.9 copy.18
  1.5 0.1 reshape_squeeze.3
  1.6 1.9 convert_reduce_fusion
  3.5 0.5 fusion.18.slots
  4.1 0.8 copy.19
  4.9 0.1 broadcast_in_dim.25
  5.0 2.0 select_reduce_fusion
  7.0 1.2 copy.20
  8.2 0.2 copy.21
  8.3 0.1 pad_maximum_fusion
  8.4 0.6 fusion.15
  9.0 0.0 copy-start.2
  9.0 1.2 copy.24
  10.2 0.1 reshape.56
  10.3 1.1 copy.22
  11.4 1.7 convolution_convert_fusion.q_ref
  13.1 108.9 %spread.1 = bf16[4,4,4,2,512,128]{5,4,3,2,1,0:T(8,128)(2,1)} custom-call(s32[8192]{0:T(1024)} %bitcast.41, bf16[4,512,128]{2,1,0:T(8,128)(2,1)} %bitcast.34), custom_call_target="tpu_custom_call" | custom-call | tf_op jit(solution)/shard_map/spread/pallas_call | solution.py:319
  122.0 32.5 %attend.1 = (bf16[512,768]{1,0:T(8,128)(2,1)}, bf16[4,4,384,128]{3,2,1,0:T(8,128)(2,1)}, bf16[4,4,384,128]{3,2,1,0:T(8,128)(2,1)}, f32[4,4,384,128]{3,2,1,0:T(8,...) custom-call(s32[64]{0:T(128)} %fusion.18.slots, bf16[512,768]{1,0:T(8,128)(2,1)} %convolution_convert_fusion.q_ref, ...), custom_call_target="tpu_custom_call" | custom-call | tf_op jit(solution)/shard_map/attend/pallas_call | solution.py:121
  154.5 131.8 %collect.1 = (bf16[512,768]{1,0:T(8,128)(2,1)}, bf16[4,4,128,128]{3,2,1,0:T(8,128)(2,1)}, bf16[4,2,2,4,2,128,128]{6,5,4,3,2,1,0:T(8,128)(2,1)}, bf16[4,2,2,4,128...) custom-call(s32[8192]{0:T(1024)} %bitcast.42, s32[128]{0:T(128)} %get-tuple-element.11.inv, ...), custom_call_target="tpu_custom_call" | custom-call | tf_op jit(solution)/shard_map/collect/pallas_call | solution.py:638
  286.4 0.0 copy-start.3
  286.4 1.6 copy.23
  288.0 0.1 copy.27
  288.1 3.2 %fusion.10 = bf16[1,512,768]{2,1,0:T(8,128)(2,1)} fusion(bf16[768,512]{1,0:T(8,128)(2,1)S(1)} %copy-done, bf16[768,768]{1,0:T(8,128)(2,1)S(1)} %copy-done.3, bf16[512,512]{1,0:T(8,128)(2,1)S(1)} %bitcast.40, bf16[512,768]{1,0:T(8,128)(2,1)} %get-tuple-element.16), kind=kOutput, calls=%fused_computation.12 | convolution fusion | flops 1013579776 | bytes 4063232 | tf_op jit(solution)/shard_map/dot_general | solution.py:680
  (9 shorter events, 0.0 us)
Async XLA Ops:
  0.6 7.5 %copy-start.1 = (bf16[768,256]{1,0:T(8,128)(2,1)S(1)}, bf16[768,256]{1,0:T(8,128)(2,1)}, u32[]{:S(2)}) copy-start(bf16[768,256]{1,0:T(8,128)(2,1)} %param.12) | copy-start | bytes 1179652
  1.5 6.9 %copy-start.4 = (bf16[1,512,768]{2,1,0:T(8,128)(2,1)S(1)}, bf16[1,512,768]{2,1,0:T(8,128)(2,1)}, u32[]{:S(2)}) copy-start(bf16[1,512,768]{2,1,0:T(8,128)(2,1)} %param.8) | copy-start | bytes 2359300
  9.0 2.4 copy-start.2
  286.4 1.7 copy-start
  286.4 1.7 copy-start.3

commit v3 on v2

--- a/solution.py
+++ b/solution.py
@@ -1,5 +1,3 @@
-import functools
-
 import jax
 import jax.numpy as jnp
 from jax import lax
@@ -7,7 +5,6 @@
 from jax.experimental.pallas import tpu as pltpu
 from jax.sharding import PartitionSpec as P
 
-CAP = 2
 LOG2E = 1.4426950408889634
 EPSILON = 1e-06
 F32, BF16 = jnp.float32, jnp.bfloat16
@@ -15,80 +12,6 @@
 
 def dot(a, b, ca=1, cb=0):
     return lax.dot_general(a, b, (((ca,), (cb,)), ((), ())), preferred_element_type=F32)
-
-
-def attend_kernel(slots, q_ref, go_ref, wo_ref, arr_ref, lay_ref, qp_ref, dop_ref, stat_ref, inv_ref, ent_ref,
-                  kv, e, acc, att, in_sem, out_sem):
-    b, nb = pl.program_id(0), pl.num_programs(0)
-    L = kv.shape[1]
-    cur = lax.rem(b, 2)
-
-    def fetch(blk, slot):
-        return [pltpu.make_async_copy(arr_ref.at[slots[blk * L + l]], kv.at[slot, l], in_sem.at[slot, l]) for l in range(L)]
-
-    def keep(blk, slot):
-        return [pltpu.make_async_copy(kv.at[slot, :, g], ent_ref.at[g, pl.ds(blk * L, L)], out_sem.at[slot, g]) for g in range(4)]
-
-    @pl.when(b == 0)
-    def _():
-        for c in fetch(0, 0):
-            c.start()
-
-    @pl.when(b >= 1)
-    def _():
-        for c in keep(b - 1, 1 - cur):
-            c.wait()
-
-    @pl.when(b + 1 < nb)
-    def _():
-        for c in fetch(b + 1, 1 - cur):
-            c.start()
-
-    @pl.when(b == 0)
-    def _():
-        def clear(i, _):
-            inv_ref[i] = 0
-            return 0
-        lax.fori_loop(0, inv_ref.shape[0], clear, 0)
-
-        def put(i, _):
-            inv_ref[slots[i]] = i
-            return 0
-        lax.fori_loop(0, nb * L, put, 0)
-
-    zero = jnp.zeros((128, 64), BF16)
-    for h in range(12):
-        x = q_ref[:, (h // 2) * 128:(h // 2) * 128 + 128][:, (h % 2) * 64:(h % 2) * 64 + 64]
-        qp_ref[h // 3, (h % 3) * 128:(h % 3) * 128 + 128, :] = jnp.concatenate([x, zero], axis=1)
-    for c in fetch(b, cur):
-        c.wait()
-    for c in keep(b, cur):
-        c.start()
-
-    for g in range(4):
-        m, inv, out = attend_rows(qp_ref[g], kv[cur, :, g].reshape(L * 128, 128), e)
-        stat_ref[g] = jnp.concatenate([m[:, :64], inv[:, 64:]], axis=1)
-        acc[g] = out
-
-    ss = jnp.zeros((128, 128), F32)
-    for j in range(6):
-        a = jnp.concatenate([acc[h // 3, (h % 3) * 128:(h % 3) * 128 + 128, :][:, 64:] for h in (2 * j, 2 * j + 1)], axis=1)
-        a = a.astype(BF16).astype(F32)
-        att[:, j * 128:j * 128 + 128] = a
-        ss = ss + a * a
-    root = jnp.sqrt(jnp.sum(ss, axis=1, keepdims=True) * (1.0 / 768) + EPSILON)
-    normed = att[...] / root
-    lay_ref[...] = dot(normed.astype(BF16), wo_ref[...]).astype(BF16)
-    ng = dot(go_ref[...], wo_ref[...], 1, 1)
-    att[...] = (ng - normed * (jnp.sum(ng * normed, axis=1, keepdims=True) * (1.0 / 768))) / root
-    for h in range(12):
-        x = att[:, (h // 2) * 128:(h // 2) * 128 + 128][:, (h % 2) * 64:(h % 2) * 64 + 64].astype(BF16)
-        dop_ref[h // 3, (h % 3) * 128:(h % 3) * 128 + 128, :] = jnp.concatenate([zero, x], axis=1)
-
-    @pl.when(b == nb - 1)
-    def _():
-        for c in keep(b, cur):
-            c.wait()
 
 
 SCALE = 0.125 * LOG2E
@@ -111,38 +34,9 @@
     return m, inv, dot(low, kv)
 
 
-def attention(slots, queries, grads, w_out, arr):
-    rows, D = queries.shape
-    nb = rows // 128
-    L = slots.shape[0] // nb
-    ns = arr.shape[0]
-    row = lambda b, s: (b, 0)
-    padded = lambda b, s: (b, 0, 0, 0)
-    return pl.pallas_call(
-        attend_kernel,
-        grid_spec=pltpu.PrefetchScalarGridSpec(
-            num_scalar_prefetch=1, grid=(nb,),
-            in_specs=[pl.BlockSpec((128, D), row), pl.BlockSpec((128, D), row),
-                      pl.BlockSpec((D, D), lambda b, s: (0, 0), pipeline_mode=pl.Buffered(1)),
-                      pl.BlockSpec(memory_space=pl.ANY)],
-            out_specs=[pl.BlockSpec((128, D), row)] + [pl.BlockSpec((None, 4, 384, 128), padded)] * 3
-                      + [pl.BlockSpec(memory_space=pltpu.SMEM), pl.BlockSpec(memory_space=pl.ANY)],
-            scratch_shapes=[
-                pltpu.VMEM((2, L, 4, 128, 128), BF16), pltpu.VMEM((384, 2048), F32),
-                pltpu.VMEM((4, 384, 128), F32), pltpu.VMEM((128, 768), F32),
-                pltpu.SemaphoreType.DMA((2, L)), pltpu.SemaphoreType.DMA((2, 4))]),
-        out_shape=[jax.ShapeDtypeStruct((rows, D), BF16), jax.ShapeDtypeStruct((nb, 4, 384, 128), BF16),
-                   jax.ShapeDtypeStruct((nb, 4, 384, 128), BF16), jax.ShapeDtypeStruct((nb, 4, 384, 128), F32),
-                   jax.ShapeDtypeStruct((ns,), jnp.int32), jax.ShapeDtypeStruct((4, nb * L, 128, 128), BF16)],
-        compiler_params=pltpu.CompilerParams(dimension_semantics=("arbitrary",), vmem_limit_bytes=60 * 2**20),
-        name="attend",
-    )(slots, queries, grads, w_out, arr.reshape(ns, 4, 128, 128))
-
-
 MESH = pl.DeviceIdType.MESH
 SIDE = 4
 ORDERS = ((0, 1, 2), (1, 2, 0), (2, 0, 1))
-PIECES = ((0, 176), (176, 176), (352, 160))
 STRIDE = (16, 4, 1)
 
 
@@ -193,54 +87,126 @@
     return ref.at[tuple(index if d == axis else slice(None) for d in dims) + rest]
 
 
-def spread_kernel(wanted, mine_ref, out_ref, own, plane0, plane1, plane2, st0, st1, st2, rl0, rl1, rl2,
-                  send_sem, recv_sem, swap_sem, local_sem):
+CUTS = ((48, 48, 32), (48, 32, 48), (32, 48, 48), (48, 48, 32))
+
+
+def spans(g):
+    start = 0
+    out = []
+    for rows in CUTS[g]:
+        out.append((start, rows))
+        start += rows
+    return out
+
+
+def offset(g, p):
+    return sum(CUTS[i][p] for i in range(g))
+
+
+def forward_kernel(tok_ref, go_ref, wq_ref, wk_ref, wv_ref, wo_ref, kt_ref, kb_ref,
+                   lay_ref, qp_ref, dop_ref, stat_ref, ent_ref, want_ref, inv_ref, rl_ref,
+                   mine, own, plane0, plane1, plane2, stage, arr0, arr1, arr2, arr3, e, kvb, qv, dov, stv, att, ng, lay,
+                   named, ranks, wtab, itab, stab, want, slot,
+                   send_sem, recv_sem, swap_sem, local_sem, tab_sem, ent_sem, out_sem):
     pos, core = place(), lax.axis_index("vintage")
-    planes, stages, relays = (plane0, plane1, plane2), (st0, st1, st2), (rl0, rl1, rl2)
-    greet(pos, core)
+    me = tile_of(pos)
+    planes, arr = (plane0, plane1, plane2), (arr0, arr1, arr2, arr3)
+    dims = [tuple(sorted(o[:2])) for o in ORDERS]
+    send = Sender(pos, core, send_sem, recv_sem)
+    nb, L = 4, 16
+    greet(pos, core, False)
+
+    k = dot(tok_ref[...], wk_ref[...]).astype(BF16)
+    v = dot(tok_ref[...], wv_ref[...]).astype(BF16)
+    for g in range(4):
+        both = jnp.concatenate([k[:, g * 64:g * 64 + 64], v[:, g * 64:g * 64 + 64]], axis=1)
+        for b in range(nb):
+            mine[b, g * 128:g * 128 + 128, :] = both[b * 128:b * 128 + 128]
+
+    lane = lax.broadcasted_iota(jnp.int32, (256, 128), 1)
+    tile = jnp.where(lane < 64, lane, lane - 64)
+    row = lax.broadcasted_iota(jnp.int32, (256, 128), 0)
+    quarter = row - (row // 4) * 4
+    block, entry = jnp.zeros((256, 128), jnp.int32), jnp.zeros((256, 128), jnp.int32)
+    for l in range(L):
+        hit = kt_ref[:, l:l + 1] == tile
+        block = jnp.where(hit, kb_ref[:, l:l + 1] + 1, block)
+        entry = jnp.where(hit, quarter * L + l + 1, entry)
+    lane4 = lax.broadcasted_iota(jnp.int32, (64, 128), 1)
+    for source, table in ((block, wtab), (entry, itab)):
+        named[...] = source
+        one, two = jnp.zeros((64, 128), jnp.int32), jnp.zeros((64, 128), jnp.int32)
+        for i in range(4):
+            x = named[pl.ds(i, 64, stride=4), :]
+            ranks[pl.ds(i, 64, stride=4), :] = jnp.where(one > 0, 1, 0)
+            two = jnp.where((one > 0) & (x > 0), x, two)
+            one = jnp.where(one > 0, one, x)
+        table[...] = jnp.where(lane4 < 64, one, two) - 1
+    itab[...] = jnp.maximum(itab[...], 0)
+    half = pl.ds(pl.multiple_of(lax.div(me, 2) * 8, 8), 8)
+    mine_kt, mine_rank = kt_ref[half, :], ranks[half, :]
+    lane8 = lax.broadcasted_iota(jnp.int32, (8, 128), 1)
+    found = jnp.zeros((8, 128), jnp.int32)
+    for l in range(L):
+        at = jnp.sum(jnp.where((mine_kt[:, l:l + 1] == lane8) & (lane8 < 64), lane8 * 2 + mine_rank, 0), axis=1, keepdims=True)
+        found = jnp.where(lane8 == l, at, found)
+    stab[...] = found
+    tables = [pltpu.make_async_copy(wtab, want, tab_sem.at[0]), pltpu.make_async_copy(stab, slot, tab_sem.at[1]),
+              pltpu.make_async_copy(wtab, want_ref, tab_sem.at[2]), pltpu.make_async_copy(itab, inv_ref, tab_sem.at[3])]
+    for c in tables:
+        c.start()
+
+    greet_wait()
     swap = pltpu.make_async_remote_copy(
-        src_ref=mine_ref, dst_ref=own, send_sem=swap_sem.at[0], recv_sem=swap_sem.at[1],
-        device_id=(1 - core, tile_of(pos)), device_id_type=MESH)
+        src_ref=mine, dst_ref=own, send_sem=swap_sem.at[0], recv_sem=swap_sem.at[1],
+        device_id=(1 - core, me), device_id_type=MESH)
     swap.start()
+
+    zero = jnp.zeros((128, 64), BF16)
+    q = dot(tok_ref[...], wq_ref[...]).astype(BF16)
+    for b in range(nb):
+        for h in range(12):
+            x = q[b * 128:b * 128 + 128, (h // 2) * 128:(h // 2) * 128 + 128][:, (h % 2) * 64:(h % 2) * 64 + 64]
+            qv[b, h // 3, (h % 3) * 128:(h % 3) * 128 + 128, :] = jnp.concatenate([x, zero], axis=1)
+    outs = [pltpu.make_async_copy(qv, qp_ref, out_sem.at[0])]
+    outs[0].start()
     swap.wait()
-    send = Sender(pos, core, send_sem, recv_sem)
-    dims = [tuple(sorted(o[:2])) for o in ORDERS]
-    local = []
-
-    def line(p, axis):
-        return at_axis(planes[p], dims[p], pos[axis], axis)
 
     def cell(p, a1, i1, a2, i2, *rest):
         return planes[p].at[tuple(i1 if d == a1 else i2 for d in dims[p]) + rest]
 
-    for p, (r0, rows) in enumerate(PIECES):
-        a1, a2, a3 = ORDERS[p]
-        c = pltpu.make_async_copy(own.at[:, pl.ds(r0, rows), :], cell(p, a1, pos[a1], a2, pos[a2]), local_sem.at[p])
-        c.start()
-        local.append(c)
-    first = []
+    local = []
     for p in range(3):
         a1, a2, a3 = ORDERS[p]
-        local[p].wait()
+        for g in range(4):
+            r0, rows = spans(g)[p]
+            c = pltpu.make_async_copy(own.at[:, pl.ds(g * 128 + r0, rows), :],
+                                      cell(p, a1, pos[a1], a2, pos[a2], slice(None), pl.ds(offset(g, p), rows), slice(None)),
+                                      local_sem.at[p * 4 + g])
+            c.start()
+            local.append(c)
+    first, second, third, fourth = [], [], [], []
+    for p in range(3):
+        a1, a2, a3 = ORDERS[p]
+        for c in local[p * 4:p * 4 + 4]:
+            c.wait()
         here = cell(p, a1, pos[a1], a2, pos[a2])
-        first.append([send.copy(here, here, p * 12 + i, a1, by) for i, by in enumerate((1, 3))])
-    second = []
+        first.append([send.copy(here, here, p * 8 + i, a1, by) for i, by in enumerate((1, 3))])
     for p in range(3):
         a1, a2, a3 = ORDERS[p]
         got = []
         for i, by in enumerate((1, 3)):
             first[p][i].wait_recv()
             part = cell(p, a1, lax.rem(pos[a1] + SIDE - by, SIDE), a2, pos[a2], pl.ds(2 * i, 2))
-            got.append(send.copy(part, part, p * 12 + 2 + i, a1, by))
+            got.append(send.copy(part, part, p * 8 + 2 + i, a1, by))
         second.append(got)
-    third = []
     for p in range(3):
         a1, a2, a3 = ORDERS[p]
         for c in second[p]:
             c.wait_recv()
-        here = line(p, a2)
-        third.append([send.copy(here, here, p * 12 + 4 + i, a2, by) for i, by in enumerate((1, 3))])
-    fourth = []
+        here = planes[p].at[tuple(pos[a2] if d == a2 else slice(None) for d in dims[p])]
+        third.append([send.copy(here, here, p * 8 + 4 + i, a2, by) for i, by in enumerate((1, 3))])
+    ng[...] = dot(go_ref[...], wo_ref[...], 1, 1)
     for p in range(3):
         a1, a2, a3 = ORDERS[p]
         got = []
@@ -248,12 +214,12 @@
             third[p][i].wait_recv()
             other = lax.rem(pos[a2] + SIDE - by, SIDE)
             part = planes[p].at[tuple(other if d == a2 else pl.ds(2 * i, 2) for d in dims[p])]
-            got.append(send.copy(part, part, p * 12 + 6 + i, a2, by))
+            got.append(send.copy(part, part, p * 8 + 6 + i, a2, by))
         fourth.append(got)
 
-    def landing(p, source, half=None):
+    def landing(g, p, source, half=None):
         a3 = ORDERS[p][2]
-        r0, rows = PIECES[p]
+        r0, rows = spans(g)[p]
         idx = []
         for d in range(3):
             if d == a3:
@@ -262,90 +228,174 @@
                 idx.append(pl.ds(2 * half, 2))
             else:
                 idx.append(slice(None))
-        return out_ref.at[tuple(idx) + (slice(None), pl.ds(r0, rows), slice(None))]
-
-    fifth = []
-    for p in range(3):
-        a1, a2, a3 = ORDERS[p]
-        r0, rows = PIECES[p]
-        for c in fourth[p]:
+        return arr[g].at[tuple(idx) + (slice(None), pl.ds(r0, rows), slice(None))]
+
+    def pick(g, p, k, by):
+        a3 = ORDERS[p][2]
+        r0, rows = spans(g)[p]
+        dest = tile_of(shifted(pos, a3, by))
+
+        def one(j, _):
+            hi, lo = lax.div(j, SIDE), lax.rem(j, SIDE)
+            source = pos[a3] * STRIDE[a3] + hi * STRIDE[dims[p][0]] + lo * STRIDE[dims[p][1]]
+            where = [None] * 3
+            where[a3], where[dims[p][0]], where[dims[p][1]] = pos[a3], hi, lo
+            for s in range(2):
+                blk = jnp.maximum(want[dest, s * 64 + source], 0)
+                val = planes[p][hi, lo, blk, pl.ds(offset(g, p), rows), :]
+                if k < 3:
+                    stage[k, hi, lo, s, pl.ds(g * 128 + r0, rows), :] = val
+                else:
+                    arr[g][tuple(where) + (s, pl.ds(r0, rows), slice(None))] = val
+            return 0
+        lax.fori_loop(0, SIDE * SIDE, one, 0)
+
+    rows_of = lambda g, p: (slice(None), pl.ds(g * 128 + spans(g)[p][0], spans(g)[p][1]), slice(None))
+    W = slice(None)
+    zr, zd, zf = {}, {}, {}
+
+    def z_send(g):
+        zr[g], zd[g] = [], []
+        for p in range(3):
+            a3 = ORDERS[p][2]
+            if g == 0:
+                for c in fourth[p]:
+                    c.wait_recv()
+            pick(g, p, 2, 2)
+            for i, by in enumerate((1, 3)):
+                zr[g].append(send.copy(stage.at[(2, pl.ds(2 * i, 2), W) + rows_of(g, p)], rl_ref.at[(i, W, W) + rows_of(g, p)],
+                                       24 + (g * 3 + p) * 6 + i, a3, by))
+        for p in range(3):
+            a3 = ORDERS[p][2]
+            for i, by in enumerate((1, 3)):
+                pick(g, p, i, by)
+                zd[g].append(send.copy(stage.at[(i, W, W) + rows_of(g, p)], landing(g, p, pos[a3]),
+                                       24 + (g * 3 + p) * 6 + 2 + i, a3, by))
+
+    def z_own(g):
+        for p in range(3):
+            pick(g, p, 3, 0)
+
+    def z_relay(g):
+        zf[g] = []
+        for p in range(3):
+            a3 = ORDERS[p][2]
+            for i, by in enumerate((1, 3)):
+                zr[g][p * 2 + i].wait_recv()
+                zf[g].append(send.copy(rl_ref.at[(i, W, W) + rows_of(g, p)], landing(g, p, lax.rem(pos[a3] + SIDE - by, SIDE), i),
+                                       24 + (g * 3 + p) * 6 + 4 + i, a3, by))
+
+    def entries(g, b, cur):
+        return pltpu.make_async_copy(kvb.at[cur], ent_ref.at[g, pl.ds(b * L, L)], ent_sem.at[cur])
+
+    base = lax.rem(me, 2) * 4
+
+    def forward(g):
+        for c in zd[g] + zf[g]:
             c.wait_recv()
 
-        def pick(k, by, p=p, a3=a3):
-            dest = tile_of(shifted(pos, a3, by))
-
-            def one(j, _):
-                hi, lo = lax.div(j, SIDE), lax.rem(j, SIDE)
-                source = pos[a3] * STRIDE[a3] + hi * STRIDE[dims[p][0]] + lo * STRIDE[dims[p][1]]
-                for s in range(2):
-                    blk = jnp.maximum(wanted[dest * 128 + s * 64 + source], 0)
-                    stages[p][k, hi, lo, s] = planes[p][hi, lo, blk]
-                return 0
-            lax.fori_loop(0, SIDE * SIDE, one, 0)
-
-        got = []
-        pick(2, 2)
-        for i, by in enumerate((1, 3)):
-            got.append(send.copy(stages[p].at[2, pl.ds(2 * i, 2)], relays[p].at[i], p * 12 + 8 + i, a3, by))
-        for i, by in enumerate((1, 3)):
-            pick(i, by)
-            send.copy(stages[p].at[i], landing(p, pos[a3]), 36 + p * 2 + i, a3, by)
-        pick(3, 0)
-        c = pltpu.make_async_copy(stages[p].at[3], landing(p, pos[a3]), local_sem.at[3 + p])
+        def one(b, _):
+            cur = lax.rem(b, 2)
+            if g == 0:
+                @pl.when(b >= 2)
+                def _():
+                    entries(g, b, cur).wait()
+            else:
+                entries(g, b, cur).wait()
+            for l in range(L):
+                at = slot[base + b, l]
+                pair, s = lax.div(at, 2), lax.rem(at, 2)
+                x, yz = lax.div(pair, 16), lax.rem(pair, 16)
+                kvb[cur, l] = arr[g][x, lax.div(yz, 4), lax.rem(yz, 4), s]
+            m, inv, out = attend_rows(qv[b, g], kvb[cur].reshape(L * 128, 128), e)
+            entries(g, b, cur).start()
+            stv[b, g] = jnp.concatenate([m[:, :64], inv[:, 64:]], axis=1)
+            att[b, g] = out.astype(BF16)
+            return 0
+        lax.fori_loop(0, nb, one, 0)
+        c = pltpu.make_async_copy(stv.at[:, g], stat_ref.at[:, g], out_sem.at[1 + g])
         c.start()
-        local.append(c)
-        fifth.append(got)
-    for p in range(3):
-        a3 = ORDERS[p][2]
-        for i, by in enumerate((1, 3)):
-            fifth[p][i].wait_recv()
-            send.copy(relays[p].at[i], landing(p, lax.rem(pos[a3] + SIDE - by, SIDE), i), p * 12 + 10 + i, a3, by)
-    for c in local[3:]:
+        outs.append(c)
+
+    tables[0].wait()
+    tables[1].wait()
+    z_send(0)
+    z_send(1)
+    z_own(0)
+    z_relay(0)
+    z_send(2)
+    z_own(1)
+    z_relay(1)
+    z_send(3)
+    forward(0)
+    z_own(2)
+    z_relay(2)
+    forward(1)
+    z_own(3)
+    z_relay(3)
+    forward(2)
+    forward(3)
+
+    for b in range(nb):
+        rows = slice(b * 128, b * 128 + 128)
+        a = []
+        for j in range(6):
+            a.append(jnp.concatenate([att[b, h // 3, (h % 3) * 128:(h % 3) * 128 + 128, :][:, 64:] for h in (2 * j, 2 * j + 1)], axis=1))
+        a = jnp.concatenate(a, axis=1).astype(F32)
+        root = jnp.sqrt(jnp.sum(a * a, axis=1, keepdims=True) * (1.0 / 768) + EPSILON)
+        normed = a / root
+        lay[rows, :] = dot(normed.astype(BF16), wo_ref[...]).astype(BF16)
+        n = ng[rows, :]
+        a = ((n - normed * (jnp.sum(n * normed, axis=1, keepdims=True) * (1.0 / 768))) / root).astype(BF16)
+        for h in range(12):
+            x = a[:, (h // 2) * 128:(h // 2) * 128 + 128][:, (h % 2) * 64:(h % 2) * 64 + 64]
+            dov[b, h // 3, (h % 3) * 128:(h % 3) * 128 + 128, :] = jnp.concatenate([zero, x], axis=1)
+    for i, (src, dst) in enumerate(((dov, dop_ref), (lay, lay_ref))):
+        c = pltpu.make_async_copy(src, dst, out_sem.at[5 + i])
+        c.start()
+        outs.append(c)
+    for b in (nb - 2, nb - 1):
+        entries(3, b, b % 2).wait()
+    for c in outs + tables[2:]:
         c.wait()
     for c in send.done:
         c.wait_send()
-    waited = set(id(c) for group in (first, second, third, fourth, fifth) for cs in group for c in cs)
-    for c in send.done:
-        if id(c) not in waited:
-            c.wait_recv()
-
-
-def spread(wanted, mine):
-    scratch = [pltpu.VMEM((4, 512, 128), BF16)]
-    for make in (lambda r: (4, 4, 4, r, 128), lambda r: (4, 4, 4, 2, r, 128), lambda r: (2, 2, 4, 2, r, 128)):
-        scratch += [pltpu.VMEM(make(rows), BF16) for _, rows in PIECES]
-    scratch += [pltpu.SemaphoreType.DMA((42,)), pltpu.SemaphoreType.DMA((42,)), pltpu.SemaphoreType.DMA((2,)),
-                pltpu.SemaphoreType.DMA((6,))]
-    return pl.pallas_call(
-        spread_kernel,
-        in_specs=[pl.BlockSpec(memory_space=pltpu.SMEM), pl.BlockSpec(memory_space=pl.ANY)],
-        out_specs=pl.BlockSpec(memory_space=pl.ANY),
-        out_shape=jax.ShapeDtypeStruct((4, 4, 4, 2, 512, 128), BF16),
-        scratch_shapes=scratch,
-        compiler_params=pltpu.CompilerParams(collective_id=0, has_side_effects=True, vmem_limit_bytes=56 * 2**20),
-        name="spread",
-    )(wanted, mine)
-
-
-CUTS = ((48, 48, 32), (48, 32, 48), (32, 48, 48), (48, 48, 32))
-
-
-def spans(g):
-    start = 0
-    out = []
-    for rows in CUTS[g]:
-        out.append((start, rows))
-        start += rows
-    return out
+
+
+def forward_pass(tokens, grads, w_query, w_key, w_value, w_out, named, blocks):
+    V, A = pl.BlockSpec(memory_space=pltpu.VMEM), pl.BlockSpec(memory_space=pl.ANY)
+    bf = lambda *shape: jax.ShapeDtypeStruct(shape, BF16)
+    i32 = lambda *shape: jax.ShapeDtypeStruct(shape, jnp.int32)
+    vm = lambda *shape: pltpu.VMEM(shape, BF16)
+    vi = lambda *shape: pltpu.VMEM(shape, jnp.int32)
+    dma = lambda *shape: pltpu.SemaphoreType.DMA(shape)
+    out = pl.pallas_call(
+        forward_kernel,
+        in_specs=[V] * 8,
+        out_specs=[A] * 8,
+        out_shape=[bf(512, 768), bf(4, 4, 384, 128), bf(4, 4, 384, 128), jax.ShapeDtypeStruct((4, 4, 384, 128), F32),
+                   bf(4, 64, 128, 128), i32(64, 128), i32(64, 128), bf(2, 2, 4, 2, 512, 128)],
+        scratch_shapes=[vm(4, 512, 128), vm(4, 512, 128)] + [vm(4, 4, 4, sum(c[p] for c in CUTS), 128) for p in range(3)] + [
+            vm(3, 4, 4, 2, 512, 128)] + [vm(4, 4, 4, 2, 128, 128)] * 4 + [pltpu.VMEM((384, 2048), F32), vm(2, 16, 128, 128),
+            vm(4, 4, 384, 128), vm(4, 4, 384, 128), pltpu.VMEM((4, 4, 384, 128), F32), vm(4, 4, 384, 128),
+            pltpu.VMEM((512, 768), F32), vm(512, 768),
+            vi(256, 128), vi(256, 128), vi(64, 128), vi(64, 128), vi(8, 128),
+            pltpu.SMEM((64, 128), jnp.int32), pltpu.SMEM((8, 128), jnp.int32),
+            dma(96), dma(96), dma(2), dma(12), dma(4), dma(2), dma(7)],
+        compiler_params=pltpu.CompilerParams(collective_id=0, has_side_effects=True, vmem_limit_bytes=67043328),
+        name="forward",
+    )(tokens, grads, w_query, w_key, w_value, w_out, named, blocks)
+    return out[:7]
 
 
 def return_kernel(wanted, inv, qp_ref, dop_ref, stat_ref, ent_ref, dq_ref, out_ref, rl_ref, yl_ref, xl_ref,
-                  kvb, p, t, dqs, parts, stage, rz, sums, gs, ys, hs, xs, total,
-                  send_sem, recv_sem, swap_sem, kv_sem):
+                  kvb, qv, dov, stv, p, t, dqs, parts, stage, rz, sums, gs, ys, hs, xs, total,
+                  send_sem, recv_sem, swap_sem, kv_sem, in_sem):
     pos, core = place(), lax.axis_index("vintage")
     dims = [tuple(sorted(o[:2])) for o in ORDERS]
     send = Sender(pos, core, send_sem, recv_sem)
-    nb = qp_ref.shape[0]
+    nb = qv.shape[0]
+    me = tile_of(pos)
     L = kvb.shape[1]
     greet(pos, core, False)
 
@@ -359,8 +409,18 @@
         return pltpu.make_async_copy(ent_ref.at[g, pl.ds(b * L, L)], kvb.at[slot], kv_sem.at[slot])
 
     load(0, 0, 0).start()
+    rows_in = [[pltpu.make_async_copy(src.at[:, g], dst.at[:, g], in_sem.at[g, i])
+                for i, (src, dst) in enumerate(((qp_ref, qv), (dop_ref, dov), (stat_ref, stv)))] for g in range(4)]
+    for c in rows_in[0]:
+        c.start()
 
     def backward(g):
+        for c in rows_in[g]:
+            c.wait()
+        if g < 3:
+            for c in rows_in[g + 1]:
+                c.start()
+
         def one(b, _):
             cur = lax.rem(b, 2)
             load(g, b, cur).wait()
@@ -375,9 +435,9 @@
                     load(g + 1, 0, 0).start()
 
             kv = kvb[cur].reshape(L * 128, 128)
-            q, do = qp_ref[b, g], dop_ref[b, g]
-            m = jnp.broadcast_to(stat_ref[b, g, :, 0:1], (384, 128))
-            nrm = jnp.broadcast_to(stat_ref[b, g, :, 64:65], (384, 128))
+            q, do = qv[b, g], dov[b, g]
+            m = jnp.broadcast_to(stv[b, g, :, 0:1], (384, 128))
+            nrm = jnp.broadcast_to(stv[b, g, :, 64:65], (384, 128))
             s = dot(q, kv, 1, 1)
             dp = dot((do.astype(F32) * 0.125).astype(BF16), kv, 1, 1)
             rd = jnp.zeros((384, 128), F32)
@@ -431,7 +491,7 @@
         def place_part(j, _):
             x, y, z = lax.div(j, 16), lax.rem(lax.div(j, 4), 4), lax.rem(j, 4)
             for s in range(2):
-                stage[g % 2, x, y, z, s] = parts[inv[j * 2 + s]]
+                stage[g % 2, x, y, z, s] = parts[inv[me, s * 64 + j]]
             return 0
         lax.fori_loop(0, 64, place_part, 0)
         if g == 0:
@@ -470,7 +530,7 @@
                 at = (k, hi, lo, s) if k < 3 else tuple(where) + (s,)
                 ref, lead = (rz, g) if k < 3 else (stage, g % 2)
                 vals.append(ref[(lead,) + at + (pl.ds(r0, rows), slice(None))].astype(F32))
-            want = [wanted[source * 128 + s * 64 + holder] for s in range(2)]
+            want = [wanted[source, s * 64 + holder] for s in range(2)]
             for b in range(4):
                 x = jnp.where(want[0] == b, vals[0], 0.0) + jnp.where(want[1] == b, vals[1], 0.0)
                 if not first:
@@ -637,16 +697,17 @@
     vm = lambda *shape: pltpu.VMEM(shape, BF16)
     out = pl.pallas_call(
         return_kernel,
-        in_specs=[S, S, V, V, V, A],
+        in_specs=[S, S, A, A, A, A],
         out_specs=[V, A, A, A, A],
         out_shape=[bf(512, 768), bf(4, 4, 128, 128), bf(4, 2, 2, 4, 2, 128, 128), bf(4, 2, 2, 4, 128, 128), bf(4, 2, 2, 128, 128)],
         scratch_shapes=[
-            vm(2, 16, 128, 128), pltpu.VMEM((384, 2048), F32), pltpu.VMEM((384, 2048), F32), vm(4, 4, 384, 128),
+            vm(2, 16, 128, 128), vm(4, 4, 384, 128), vm(4, 4, 384, 128), pltpu.VMEM((4, 4, 384, 128), F32),
+            pltpu.VMEM((384, 2048), F32), pltpu.VMEM((384, 2048), F32), vm(4, 4, 384, 128),
             vm(64, 128, 128), vm(2, 4, 4, 4, 2, 128, 128), vm(4, 3, 4, 4, 2, 128, 128),
             pltpu.VMEM((4, 4, 4, 128, 128), F32), vm(4, 4, 4, 4, 128, 128), vm(4, 3, 4, 4, 128, 128),
             vm(4, 4, 4, 128, 128), vm(4, 3, 4, 128, 128), vm(4, 4, 128, 128),
             pltpu.SemaphoreType.DMA((216,)), pltpu.SemaphoreType.DMA((216,)), pltpu.SemaphoreType.DMA((2, 4)),
-            pltpu.SemaphoreType.DMA((2,))],
+            pltpu.SemaphoreType.DMA((2,)), pltpu.SemaphoreType.DMA((4, 3))],
         compiler_params=pltpu.CompilerParams(collective_id=1, has_side_effects=True, vmem_limit_bytes=67043328),
         name="collect",
     )(wanted, inv, qp, dop, stat, ent)
@@ -654,29 +715,13 @@
 
 
 def shards(patches, out_grad, w_query, w_key, w_value, w_out, key_tiles, key_blocks):
-    tokens, grads_in = patches[0], out_grad[0]
-    my_tile = lax.axis_index("tile")
-    tiles = lax.axis_size("tile")
-    named = key_tiles[0].reshape(tiles, -1)
-    blocks = key_blocks[0].reshape(tiles, -1)
-    entries = named.shape[1]
-    earlier = jnp.arange(entries)[None, :] < jnp.arange(entries)[:, None]
-    rank = jnp.sum(((named[:, :, None] == named[:, None, :]) & earlier[None]).astype(jnp.int32), axis=2)
-    place_of = rank * tiles + named
-    hits = place_of[:, :, None] == jnp.arange(CAP * tiles, dtype=jnp.int32)[None, None, :]
-    wanted = jnp.max(jnp.where(hits, blocks[:, :, None], -1), axis=1).reshape(-1)
-    slots = lax.dynamic_slice_in_dim(named * CAP + rank, my_tile, 1, 0).reshape(-1)
-
     w_kv = jnp.concatenate([w_key.reshape(-1, 4, 64), w_value.reshape(-1, 4, 64)], axis=2).reshape(-1, 512)
-    kv = jnp.dot(tokens, w_kv, preferred_element_type=jnp.float32).astype(jnp.bfloat16)
-    mine = kv.reshape(4, 128, 4, 128).transpose(0, 2, 1, 3).reshape(4, 512, 128)
-    queries = jnp.dot(tokens, w_query, preferred_element_type=jnp.float32).astype(jnp.bfloat16)
-    arrived = spread(wanted, mine)
-    layer, qp, dop, stat, inv, ent = attention(slots, queries, grads_in, w_out, arrived.reshape(tiles * CAP, 512, 128))
+    rhs = jnp.concatenate([w_query, w_kv], axis=1)
+    layer, qp, dop, stat, ent, wanted, inv = forward_pass(
+        patches[0], out_grad[0], w_query, w_key, w_value, w_out, key_tiles[0], key_blocks[0])
     query_grad, kv_grad = gather_back(wanted, inv, qp, dop, stat, ent)
     kv_grad = kv_grad.transpose(1, 2, 0, 3).reshape(512, 512)
     lhs = jnp.concatenate([query_grad, kv_grad], axis=1)
-    rhs = jnp.concatenate([w_query, w_kv], axis=1)
     total = lax.dot_general(lhs, rhs, (((1,), (1,)), ((), ())), preferred_element_type=jnp.float32)
     return layer[None], total.astype(jnp.bfloat16)[None]
 

time: 292 us -> 272 us (0.932)
  Pallas kernels: 273 us -> 260 us
  other arithmetic: 4.49 us -> 0.05 us
    pallas_call x3 -> x2, Pallas kernels: 273 us -> 260 us  [the longest x1 131 us: gather_back(): pl.pallas_call(return_kernel, in_specs=[S, S, A, A, A, A], out_specs=[V,...]
where the time goes in v3:
time: 272 us
  Pallas kernels  260 us (96%)
  local copies, waits for them, and re-layouts  7.6 us (3%)
  matrix products  3.46 us (1%)
    pallas_call x1, Pallas kernels, gather_back(): pl.pallas_call(return_kernel, in_specs=[S, S, A, A, A, A], out_specs=[V,...  131 us
    pallas_call x1, Pallas kernels, forward_pass(): pl.pallas_call(forward_kernel, in_specs=[V] * 8, out_specs=[A] * 8, out_s...  128 us
    unnamed x14, local copies, waits for them, and re-layouts  5.8 us

profile of v3, /device:TPU:1, one launch (start us, length us, event | category | flops | bytes accessed | tf_op | source)
XLA Modules:
  0.0 271.7 jit_solution(979947474614820098)
XLA Ops:
  0.6 1.5 copy.12
  2.1 1.5 copy.13
  3.6 128.5 %forward.1 = (bf16[512,768]{1,0:T(8,128)(2,1)}, bf16[4,4,384,128]{3,2,1,0:T(8,128)(2,1)}, bf16[4,4,384,128]{3,2,1,0:T(8,128)(2,1)}, f32[4,4,384,128]{3,2,1,0:T(8...) custom-call(bf16[512,768]{1,0:T(8,128)(2,1)} %bitcast.20, ...), custom_call_target="tpu_custom_call" | custom-call | tf_op jit(solution)/shard_map/forward/pallas_call | solution.py:372
  132.1 131.4 %collect.1 = (bf16[512,768]{1,0:T(8,128)(2,1)}, bf16[4,4,128,128]{3,2,1,0:T(8,128)(2,1)}, bf16[4,2,2,4,2,128,128]{6,5,4,3,2,1,0:T(8,128)(2,1)}, bf16[4,2,2,4,128...) custom-call(s32[64,128]{1,0:T(8,128)} %get-tuple-element.12.wanted, s32[64,128]{1,0:T(8,128)} %get-tuple-element.13.inv, ...), custom_call_target="tpu_custom_call" | custom-call | tf_op jit(solution)/shard_map/collect/pallas_call | solution.py:698
  263.5 0.0 copy-start
  263.5 0.0 copy-start.1
  263.5 1.5 copy.14
  265.0 0.9 copy.20
  265.9 0.0 copy-done
  265.9 0.2 copy.15
  266.1 0.0 copy-done.1
  266.1 0.0 copy-start.2
  266.1 0.2 copy.16
  266.3 0.1 pad_maximum_fusion
  266.3 0.3 copy.17
  266.6 0.7 copy-done.2
  267.4 0.0 copy-start.3
  267.4 3.5 %fusion.10 = bf16[1,512,768]{2,1,0:T(8,128)(2,1)} fusion(bf16[768,512]{1,0:T(8,128)(2,1)S(1)} %copy.17, bf16[768,768]{1,0:T(8,128)(2,1)S(1)} %copy-done.2, bf16[512,512]{1,0:T(8,128)(2,1)} %bitcast.26, bf16[512,768]{1,0:T(8,128)(2,1)} %get-tuple-element.18), kind=kOutput, calls=%fused_computation.8 | convolution fusion | flops 1013579776 | bytes 4063232 | tf_op jit(solution)/shard_map/dot_general | solution.py:725
  270.8 0.0 copy-done.3
  270.8 0.9 copy.22
Async XLA Ops:
  263.5 2.4 copy-start
  263.5 2.6 copy-start.1
  266.1 1.3 copy-start.2
  267.4 3.5 %copy-start.3 = (bf16[512,768]{1,0:T(8,128)(2,1)S(1)}, bf16[512,768]{1,0:T(8,128)(2,1)}, u32[]{:S(2)}) copy-start(bf16[512,768]{1,0:T(8,128)(2,1)} %get-tuple-element.11) | copy-start | bytes 2359300

commit v4 on v3

--- a/solution.py
+++ b/solution.py
@@ -100,17 +100,17 @@
 
 
 def offset(g, p):
-    return sum(CUTS[i][p] for i in range(g))
+    return sum(CUTS[i][p] for i in range(g - g % 2, g))
 
 
 def forward_kernel(tok_ref, go_ref, wq_ref, wk_ref, wv_ref, wo_ref, kt_ref, kb_ref,
                    lay_ref, qp_ref, dop_ref, stat_ref, ent_ref, want_ref, inv_ref, rl_ref,
-                   mine, own, plane0, plane1, plane2, stage, arr0, arr1, arr2, arr3, e, kvb, qv, dov, stv, att, ng, lay,
-                   named, ranks, wtab, itab, stab, want, slot,
+                   mine, own, plane0, plane1, plane2, plane3, plane4, plane5, stage, arr0, arr1, arr2, arr3, e, kvb, qv, dov, stv, att, ng, lay,
+                   named, ranks, tiles, wtab, itab, stab, want, slot,
                    send_sem, recv_sem, swap_sem, local_sem, tab_sem, ent_sem, out_sem):
     pos, core = place(), lax.axis_index("vintage")
     me = tile_of(pos)
-    planes, arr = (plane0, plane1, plane2), (arr0, arr1, arr2, arr3)
+    planes, arr = ((plane0, plane1), (plane2, plane3), (plane4, plane5)), (arr0, arr1, arr2, arr3)
     dims = [tuple(sorted(o[:2])) for o in ORDERS]
     send = Sender(pos, core, send_sem, recv_sem)
     nb, L = 4, 16
@@ -123,14 +123,47 @@
         for b in range(nb):
             mine[b, g * 128:g * 128 + 128, :] = both[b * 128:b * 128 + 128]
 
+    greet_wait()
+    swap = pltpu.make_async_remote_copy(
+        src_ref=mine, dst_ref=own, send_sem=swap_sem.at[0], recv_sem=swap_sem.at[1],
+        device_id=(1 - core, me), device_id_type=MESH)
+    swap.start()
+
+    swap.wait()
+
+    def cell(p, h, a1, i1, a2, i2, *rest):
+        return planes[p][h].at[tuple(i1 if d == a1 else i2 for d in dims[p]) + rest]
+
+    local = {}
+    for h in range(2):
+        for p in range(3):
+            a1, a2, a3 = ORDERS[p]
+            local[p, h] = []
+            for g in (2 * h, 2 * h + 1):
+                r0, rows = spans(g)[p]
+                c = pltpu.make_async_copy(own.at[:, pl.ds(g * 128 + r0, rows), :],
+                                          cell(p, h, a1, pos[a1], a2, pos[a2], slice(None), pl.ds(offset(g, p), rows), slice(None)),
+                                          local_sem.at[p * 4 + g])
+                c.start()
+                local[p, h].append(c)
+    first, second, third, fourth = {}, {}, {}, {}
+    pieces = [(p, h) for h in range(2) for p in range(3)]
+    for p, h in pieces:
+        a1, a2, a3 = ORDERS[p]
+        for c in local[p, h]:
+            c.wait()
+        here = cell(p, h, a1, pos[a1], a2, pos[a2])
+        first[p, h] = [send.copy(here, here, (h * 3 + p) * 8 + i, a1, by) for i, by in enumerate((1, 3))]
+    kt, kb = kt_ref[...].T, kb_ref[...].T
+    tiles[:, :L] = kt
     lane = lax.broadcasted_iota(jnp.int32, (256, 128), 1)
     tile = jnp.where(lane < 64, lane, lane - 64)
     row = lax.broadcasted_iota(jnp.int32, (256, 128), 0)
     quarter = row - (row // 4) * 4
     block, entry = jnp.zeros((256, 128), jnp.int32), jnp.zeros((256, 128), jnp.int32)
     for l in range(L):
-        hit = kt_ref[:, l:l + 1] == tile
-        block = jnp.where(hit, kb_ref[:, l:l + 1] + 1, block)
+        hit = kt[:, l:l + 1] == tile
+        block = jnp.where(hit, kb[:, l:l + 1] + 1, block)
         entry = jnp.where(hit, quarter * L + l + 1, entry)
     lane4 = lax.broadcasted_iota(jnp.int32, (64, 128), 1)
     for source, table in ((block, wtab), (entry, itab)):
@@ -144,7 +177,7 @@
         table[...] = jnp.where(lane4 < 64, one, two) - 1
     itab[...] = jnp.maximum(itab[...], 0)
     half = pl.ds(pl.multiple_of(lax.div(me, 2) * 8, 8), 8)
-    mine_kt, mine_rank = kt_ref[half, :], ranks[half, :]
+    mine_kt, mine_rank = tiles[half, :], ranks[half, :]
     lane8 = lax.broadcasted_iota(jnp.int32, (8, 128), 1)
     found = jnp.zeros((8, 128), jnp.int32)
     for l in range(L):
@@ -156,12 +189,19 @@
     for c in tables:
         c.start()
 
-    greet_wait()
-    swap = pltpu.make_async_remote_copy(
-        src_ref=mine, dst_ref=own, send_sem=swap_sem.at[0], recv_sem=swap_sem.at[1],
-        device_id=(1 - core, me), device_id_type=MESH)
-    swap.start()
-
+    for p, h in pieces:
+        a1, a2, a3 = ORDERS[p]
+        second[p, h] = []
+        for i, by in enumerate((1, 3)):
+            first[p, h][i].wait_recv()
+            part = cell(p, h, a1, lax.rem(pos[a1] + SIDE - by, SIDE), a2, pos[a2], pl.ds(2 * i, 2))
+            second[p, h].append(send.copy(part, part, (h * 3 + p) * 8 + 2 + i, a1, by))
+    for p, h in pieces:
+        a1, a2, a3 = ORDERS[p]
+        for c in second[p, h]:
+            c.wait_recv()
+        here = planes[p][h].at[tuple(pos[a2] if d == a2 else slice(None) for d in dims[p])]
+        third[p, h] = [send.copy(here, here, (h * 3 + p) * 8 + 4 + i, a2, by) for i, by in enumerate((1, 3))]
     zero = jnp.zeros((128, 64), BF16)
     q = dot(tok_ref[...], wq_ref[...]).astype(BF16)
     for b in range(nb):
@@ -170,52 +210,15 @@
             qv[b, h // 3, (h % 3) * 128:(h % 3) * 128 + 128, :] = jnp.concatenate([x, zero], axis=1)
     outs = [pltpu.make_async_copy(qv, qp_ref, out_sem.at[0])]
     outs[0].start()
-    swap.wait()
-
-    def cell(p, a1, i1, a2, i2, *rest):
-        return planes[p].at[tuple(i1 if d == a1 else i2 for d in dims[p]) + rest]
-
-    local = []
-    for p in range(3):
+    ng[...] = dot(go_ref[...], wo_ref[...], 1, 1)
+    for p, h in pieces:
         a1, a2, a3 = ORDERS[p]
-        for g in range(4):
-            r0, rows = spans(g)[p]
-            c = pltpu.make_async_copy(own.at[:, pl.ds(g * 128 + r0, rows), :],
-                                      cell(p, a1, pos[a1], a2, pos[a2], slice(None), pl.ds(offset(g, p), rows), slice(None)),
-                                      local_sem.at[p * 4 + g])
-            c.start()
-            local.append(c)
-    first, second, third, fourth = [], [], [], []
-    for p in range(3):
-        a1, a2, a3 = ORDERS[p]
-        for c in local[p * 4:p * 4 + 4]:
-            c.wait()
-        here = cell(p, a1, pos[a1], a2, pos[a2])
-        first.append([send.copy(here, here, p * 8 + i, a1, by) for i, by in enumerate((1, 3))])
-    for p in range(3):
-        a1, a2, a3 = ORDERS[p]
-        got = []
+        fourth[p, h] = []
         for i, by in enumerate((1, 3)):
-            first[p][i].wait_recv()
-            part = cell(p, a1, lax.rem(pos[a1] + SIDE - by, SIDE), a2, pos[a2], pl.ds(2 * i, 2))
-            got.append(send.copy(part, part, p * 8 + 2 + i, a1, by))
-        second.append(got)
-    for p in range(3):
-        a1, a2, a3 = ORDERS[p]
-        for c in second[p]:
-            c.wait_recv()
-        here = planes[p].at[tuple(pos[a2] if d == a2 else slice(None) for d in dims[p])]
-        third.append([send.copy(here, here, p * 8 + 4 + i, a2, by) for i, by in enumerate((1, 3))])
-    ng[...] = dot(go_ref[...], wo_ref[...], 1, 1)
-    for p in range(3):
-        a1, a2, a3 = ORDERS[p]
-        got = []
-        for i, by in enumerate((1, 3)):
-            third[p][i].wait_recv()
+            third[p, h][i].wait_recv()
             other = lax.rem(pos[a2] + SIDE - by, SIDE)
-            part = planes[p].at[tuple(other if d == a2 else pl.ds(2 * i, 2) for d in dims[p])]
-            got.append(send.copy(part, part, p * 8 + 6 + i, a2, by))
-        fourth.append(got)
+            part = planes[p][h].at[tuple(other if d == a2 else pl.ds(2 * i, 2) for d in dims[p])]
+            fourth[p, h].append(send.copy(part, part, (h * 3 + p) * 8 + 6 + i, a2, by))
 
     def landing(g, p, source, half=None):
         a3 = ORDERS[p][2]
@@ -242,7 +245,7 @@
             where[a3], where[dims[p][0]], where[dims[p][1]] = pos[a3], hi, lo
             for s in range(2):
                 blk = jnp.maximum(want[dest, s * 64 + source], 0)
-                val = planes[p][hi, lo, blk, pl.ds(offset(g, p), rows), :]
+                val = planes[p][g // 2][hi, lo, blk, pl.ds(offset(g, p), rows), :]
                 if k < 3:
                     stage[k, hi, lo, s, pl.ds(g * 128 + r0, rows), :] = val
                 else:
@@ -258,19 +261,19 @@
         zr[g], zd[g] = [], []
         for p in range(3):
             a3 = ORDERS[p][2]
-            if g == 0:
-                for c in fourth[p]:
+            if g % 2 == 0:
+                for c in fourth[p, g // 2]:
                     c.wait_recv()
             pick(g, p, 2, 2)
             for i, by in enumerate((1, 3)):
                 zr[g].append(send.copy(stage.at[(2, pl.ds(2 * i, 2), W) + rows_of(g, p)], rl_ref.at[(i, W, W) + rows_of(g, p)],
-                                       24 + (g * 3 + p) * 6 + i, a3, by))
+                                       48 + (g * 3 + p) * 6 + i, a3, by))
         for p in range(3):
             a3 = ORDERS[p][2]
             for i, by in enumerate((1, 3)):
                 pick(g, p, i, by)
                 zd[g].append(send.copy(stage.at[(i, W, W) + rows_of(g, p)], landing(g, p, pos[a3]),
-                                       24 + (g * 3 + p) * 6 + 2 + i, a3, by))
+                                       48 + (g * 3 + p) * 6 + 2 + i, a3, by))
 
     def z_own(g):
         for p in range(3):
@@ -283,7 +286,7 @@
             for i, by in enumerate((1, 3)):
                 zr[g][p * 2 + i].wait_recv()
                 zf[g].append(send.copy(rl_ref.at[(i, W, W) + rows_of(g, p)], landing(g, p, lax.rem(pos[a3] + SIDE - by, SIDE), i),
-                                       24 + (g * 3 + p) * 6 + 4 + i, a3, by))
+                                       48 + (g * 3 + p) * 6 + 4 + i, a3, by))
 
     def entries(g, b, cur):
         return pltpu.make_async_copy(kvb.at[cur], ent_ref.at[g, pl.ds(b * L, L)], ent_sem.at[cur])
@@ -375,22 +378,23 @@
         out_specs=[A] * 8,
         out_shape=[bf(512, 768), bf(4, 4, 384, 128), bf(4, 4, 384, 128), jax.ShapeDtypeStruct((4, 4, 384, 128), F32),
                    bf(4, 64, 128, 128), i32(64, 128), i32(64, 128), bf(2, 2, 4, 2, 512, 128)],
-        scratch_shapes=[vm(4, 512, 128), vm(4, 512, 128)] + [vm(4, 4, 4, sum(c[p] for c in CUTS), 128) for p in range(3)] + [
+        scratch_shapes=[vm(4, 512, 128), vm(4, 512, 128)] + [
+            vm(4, 4, 4, CUTS[2 * h][p] + CUTS[2 * h + 1][p], 128) for p in range(3) for h in range(2)] + [
             vm(3, 4, 4, 2, 512, 128)] + [vm(4, 4, 4, 2, 128, 128)] * 4 + [pltpu.VMEM((384, 2048), F32), vm(2, 16, 128, 128),
             vm(4, 4, 384, 128), vm(4, 4, 384, 128), pltpu.VMEM((4, 4, 384, 128), F32), vm(4, 4, 384, 128),
             pltpu.VMEM((512, 768), F32), vm(512, 768),
-            vi(256, 128), vi(256, 128), vi(64, 128), vi(64, 128), vi(8, 128),
+            vi(256, 128), vi(256, 128), vi(256, 128), vi(64, 128), vi(64, 128), vi(8, 128),
             pltpu.SMEM((64, 128), jnp.int32), pltpu.SMEM((8, 128), jnp.int32),
-            dma(96), dma(96), dma(2), dma(12), dma(4), dma(2), dma(7)],
+            dma(120), dma(120), dma(2), dma(12), dma(4), dma(2), dma(7)],
         compiler_params=pltpu.CompilerParams(collective_id=0, has_side_effects=True, vmem_limit_bytes=67043328),
         name="forward",
     )(tokens, grads, w_query, w_key, w_value, w_out, named, blocks)
     return out[:7]
 
 
-def return_kernel(wanted, inv, qp_ref, dop_ref, stat_ref, ent_ref, dq_ref, out_ref, rl_ref, yl_ref, xl_ref,
-                  kvb, qv, dov, stv, p, t, dqs, parts, stage, rz, sums, gs, ys, hs, xs, total,
-                  send_sem, recv_sem, swap_sem, kv_sem, in_sem):
+def return_kernel(wanted, inv, qp_ref, dop_ref, stat_ref, ent_ref, wq_ref, wk_ref, wv_ref, out_ref, rl_ref, yl_ref, xl_ref,
+                  kvb, qv, dov, stv, p, t, dqs, parts, stage, rz, sums, gs, ys, hs, xs, total, got, wq, flat, wkv,
+                  send_sem, recv_sem, swap_sem, kv_sem, in_sem, w_sem):
     pos, core = place(), lax.axis_index("vintage")
     dims = [tuple(sorted(o[:2])) for o in ORDERS]
     send = Sender(pos, core, send_sem, recv_sem)
@@ -409,9 +413,12 @@
         return pltpu.make_async_copy(ent_ref.at[g, pl.ds(b * L, L)], kvb.at[slot], kv_sem.at[slot])
 
     load(0, 0, 0).start()
-    rows_in = [[pltpu.make_async_copy(src.at[:, g], dst.at[:, g], in_sem.at[g, i])
+    rows_in = [[pltpu.make_async_copy(src.at[:, g], dst.at[:, g % dst.shape[1]], in_sem.at[g, i])
                 for i, (src, dst) in enumerate(((qp_ref, qv), (dop_ref, dov), (stat_ref, stv)))] for g in range(4)]
     for c in rows_in[0]:
+        c.start()
+    weights = [pltpu.make_async_copy(src, dst, w_sem.at[i]) for i, (src, dst) in enumerate(((wq_ref, wq), (wk_ref, flat.at[0:768]), (wv_ref, flat.at[768:1536])))]
+    for c in weights:
         c.start()
 
     def backward(g):
@@ -435,9 +442,9 @@
                     load(g + 1, 0, 0).start()
 
             kv = kvb[cur].reshape(L * 128, 128)
-            q, do = qv[b, g], dov[b, g]
-            m = jnp.broadcast_to(stv[b, g, :, 0:1], (384, 128))
-            nrm = jnp.broadcast_to(stv[b, g, :, 64:65], (384, 128))
+            q, do = qv[b, g % 2], dov[b, g % 2]
+            m = jnp.broadcast_to(stv[b, g % 2, :, 0:1], (384, 128))
+            nrm = jnp.broadcast_to(stv[b, g % 2, :, 64:65], (384, 128))
             s = dot(q, kv, 1, 1)
             dp = dot((do.astype(F32) * 0.125).astype(BF16), kv, 1, 1)
             rd = jnp.zeros((384, 128), F32)
@@ -634,15 +641,29 @@
                     mine = mine + xs[(g, k, b) + at].astype(F32)
                 total[(g, b) + at] = mine.astype(BF16)
         c = pltpu.make_async_remote_copy(
-            src_ref=total.at[g], dst_ref=out_ref.at[g], send_sem=swap_sem.at[0, g], recv_sem=swap_sem.at[1, g],
+            src_ref=total.at[g], dst_ref=got.at[g], send_sem=swap_sem.at[0, g], recv_sem=swap_sem.at[1, g],
             device_id=(1 - core, tile_of(pos)), device_id_type=MESH)
         c.start()
         swaps.append(c)
 
-    def queries_out(b):
-        for j in range(6):
-            dq_ref[b * 128:b * 128 + 128, j * 128:j * 128 + 128] = jnp.concatenate(
-                [dqs[b, h // 3, (h % 3) * 128:(h % 3) * 128 + 128, :][:, :64] for h in (2 * j, 2 * j + 1)], axis=1)
+    def sums_at(b):
+        return slice(b % 3 * 128, b % 3 * 128 + 128), slice(b // 3 * 768, b // 3 * 768 + 768)
+
+    def query_term(b):
+        heads = [dqs[b, h // 3, (h % 3) * 128:(h % 3) * 128 + 128, :][:, :64] for h in range(12)]
+        p[sums_at(b)] = dot(jnp.concatenate(heads, axis=1), wq[...], 1, 1)
+
+    def key_term(half):
+        for g in (2 * half, 2 * half + 1):
+            swaps[g].wait()
+        for b in range(nb):
+            both = jnp.concatenate([got[2 * half, b], got[2 * half + 1, b]], axis=1)
+            x = p[sums_at(b)] + dot(both, wkv[:, half * 256:half * 256 + 256], 1, 1)
+            if half == 0:
+                p[sums_at(b)] = x
+            else:
+                for i in range(3):
+                    flat[i * 512 + b * 128:i * 512 + b * 128 + 128, :] = x[:, i * 256:i * 256 + 256].astype(BF16)
 
     backward(0)
     z_send(0)
@@ -670,19 +691,30 @@
     y_relay(2)
     x_send(1)
     x_relay(0)
-    for b in range(4):
-        queries_out(b)
+    for c in weights:
+        c.wait()
+    for g in range(4):
+        wkv[:, g * 128:g * 128 + 128] = jnp.concatenate([flat[0:768, g * 64:g * 64 + 64], flat[768:1536, g * 64:g * 64 + 64]], axis=1)
+    query_term(0)
+    query_term(1)
     y_relay(3)
     x_send(2)
     x_relay(1)
     finish(0)
+    query_term(2)
+    query_term(3)
     x_send(3)
     x_relay(2)
     finish(1)
     x_relay(3)
     finish(2)
+    key_term(0)
     finish(3)
-    for c in swaps:
+    key_term(1)
+    results = [pltpu.make_async_copy(flat.at[i * 512:i * 512 + 512], out_ref.at[:, i * 256:i * 256 + 256], w_sem.at[3 + i]) for i in range(3)]
+    for c in results:
+        c.start()
+    for c in results:
         c.wait()
     for g in range(4):
         late = zr[g] + zd[g] if g >= 2 else []
@@ -690,40 +722,36 @@
             c.wait_send()
 
 
-def gather_back(wanted, inv, qp, dop, stat, ent):
+def gather_back(wanted, inv, qp, dop, stat, ent, w_query, w_key, w_value):
     V, A = pl.BlockSpec(memory_space=pltpu.VMEM), pl.BlockSpec(memory_space=pl.ANY)
     S = pl.BlockSpec(memory_space=pltpu.SMEM)
     bf = lambda *shape: jax.ShapeDtypeStruct(shape, BF16)
     vm = lambda *shape: pltpu.VMEM(shape, BF16)
     out = pl.pallas_call(
         return_kernel,
-        in_specs=[S, S, A, A, A, A],
-        out_specs=[V, A, A, A, A],
-        out_shape=[bf(512, 768), bf(4, 4, 128, 128), bf(4, 2, 2, 4, 2, 128, 128), bf(4, 2, 2, 4, 128, 128), bf(4, 2, 2, 128, 128)],
+        in_specs=[S, S] + [A] * 7,
+        out_specs=[A] * 4,
+        out_shape=[bf(512, 768), bf(4, 2, 2, 4, 2, 128, 128), bf(4, 2, 2, 4, 128, 128), bf(4, 2, 2, 128, 128)],
         scratch_shapes=[
-            vm(2, 16, 128, 128), vm(4, 4, 384, 128), vm(4, 4, 384, 128), pltpu.VMEM((4, 4, 384, 128), F32),
+            vm(2, 16, 128, 128), vm(4, 2, 384, 128), vm(4, 2, 384, 128), pltpu.VMEM((4, 2, 384, 128), F32),
             pltpu.VMEM((384, 2048), F32), pltpu.VMEM((384, 2048), F32), vm(4, 4, 384, 128),
             vm(64, 128, 128), vm(2, 4, 4, 4, 2, 128, 128), vm(4, 3, 4, 4, 2, 128, 128),
             pltpu.VMEM((4, 4, 4, 128, 128), F32), vm(4, 4, 4, 4, 128, 128), vm(4, 3, 4, 4, 128, 128),
-            vm(4, 4, 4, 128, 128), vm(4, 3, 4, 128, 128), vm(4, 4, 128, 128),
+            vm(4, 4, 4, 128, 128), vm(4, 3, 4, 128, 128), vm(4, 4, 128, 128), vm(4, 4, 128, 128),
+            vm(768, 768), vm(1536, 256), vm(768, 512),
             pltpu.SemaphoreType.DMA((216,)), pltpu.SemaphoreType.DMA((216,)), pltpu.SemaphoreType.DMA((2, 4)),
-            pltpu.SemaphoreType.DMA((2,)), pltpu.SemaphoreType.DMA((4, 3))],
+            pltpu.SemaphoreType.DMA((2,)), pltpu.SemaphoreType.DMA((4, 3)), pltpu.SemaphoreType.DMA((6,))],
         compiler_params=pltpu.CompilerParams(collective_id=1, has_side_effects=True, vmem_limit_bytes=67043328),
         name="collect",
-    )(wanted, inv, qp, dop, stat, ent)
-    return out[0], out[1]
+    )(wanted, inv, qp, dop, stat, ent, w_query, w_key, w_value)
+    return out[0]
 
 
 def shards(patches, out_grad, w_query, w_key, w_value, w_out, key_tiles, key_blocks):
-    w_kv = jnp.concatenate([w_key.reshape(-1, 4, 64), w_value.reshape(-1, 4, 64)], axis=2).reshape(-1, 512)
-    rhs = jnp.concatenate([w_query, w_kv], axis=1)
     layer, qp, dop, stat, ent, wanted, inv = forward_pass(
-        patches[0], out_grad[0], w_query, w_key, w_value, w_out, key_tiles[0], key_blocks[0])
-    query_grad, kv_grad = gather_back(wanted, inv, qp, dop, stat, ent)
-    kv_grad = kv_grad.transpose(1, 2, 0, 3).reshape(512, 512)
-    lhs = jnp.concatenate([query_grad, kv_grad], axis=1)
-    total = lax.dot_general(lhs, rhs, (((1,), (1,)), ((), ())), preferred_element_type=jnp.float32)
-    return layer[None], total.astype(jnp.bfloat16)[None]
+        patches[0], out_grad[0], w_query, w_key, w_value, w_out, key_tiles[0].T, key_blocks[0].T)
+    total = gather_back(wanted, inv, qp, dop, stat, ent, w_query, w_key, w_value)
+    return layer[None], total[None]
 
 
 def solution(mesh):

time: 272 us -> 262 us (0.963)
  local copies, waits for them, and re-layouts: 7.6 us -> 3.02 us
  matrix products: 3.46 us -> 0 us
    dot_general x1 -> x0, matrix products: 3.46 us -> none  [shards(): lax.dot_general(lhs, rhs, (((1,), (1,)), ((), ())), preferred_element_typ...]
    unnamed x14 -> x4, local copies, waits for them, and re-layouts: 5.8 us -> 3.02 us
where the time goes in v4:
time: 262 us; the launch traced here: 261 us
  Pallas kernels  258 us (98%)
  local copies, waits for them, and re-layouts  3.02 us (1%)
    pallas_call x1, Pallas kernels, gather_back(): pl.pallas_call(return_kernel, in_specs=[S, S] + [A] * 7, out_specs=[A] *...  132 us
    pallas_call x1, Pallas kernels, forward_pass(): pl.pallas_call(forward_kernel, in_specs=[V] * 8, out_specs=[A] * 8, out_s...  126 us

profile of v4, /device:TPU:1, one launch (start us, length us, event | category | flops | bytes accessed | tf_op | source)
XLA Modules:
  0.0 261.2 jit_solution(17837418767023157536)
XLA Ops:
  0.6 126.0 %forward.1 = (bf16[512,768]{1,0:T(8,128)(2,1)}, bf16[4,4,384,128]{3,2,1,0:T(8,128)(2,1)}, bf16[4,4,384,128]{3,2,1,0:T(8,128)(2,1)}, f32[4,4,384,128]{3,2,1,0:T(8...) custom-call(bf16[512,768]{1,0:T(8,128)(2,1)} %bitcast.10, ...), custom_call_target="tpu_custom_call" | custom-call | tf_op jit(solution)/shard_map/forward/pallas_call | solution.py:375
  126.6 131.6 %collect.1 = (bf16[512,768]{1,0:T(8,128)(2,1)}, bf16[4,2,2,4,2,128,128]{6,5,4,3,2,1,0:T(8,128)(2,1)}, bf16[4,2,2,4,128,128]{5,4,3,2,1,0:T(8,128)(2,1)}, bf16[4,2,2,128,128]{4,3,2,1,0:T(8,128)(2,1)}) custom-call(s32[64,128]{1,0:T(8,128)} %get-tuple-element.11.wanted, s32[64,128]{1,0:T(8,128)} %get-tuple-element.12.inv, ...), custom_call_target="tpu_custom_call" | custom-call | tf_op jit(solution)/shard_map/collect/pallas_call | solution.py:730
  258.2 0.0 copy-start
  258.2 2.1 copy.12
  260.4 0.0 copy-done
  260.4 0.9 copy.13
Async XLA Ops:
  258.2 2.1 copy-start

commit v5 on v4

--- a/solution.py
+++ b/solution.py
@@ -55,18 +55,19 @@
     return pos[0] * 16 + pos[1] * 4 + pos[2]
 
 
-def greet(pos, core, wait=True):
+def greet(pos, core, wait=True, beside=False):
     barrier = pltpu.get_barrier_semaphore()
     for axis in range(3):
         for by in (1, 3):
-            pl.semaphore_signal(barrier, inc=1, device_id=(core, tile_of(shifted(pos, axis, by))), device_id_type=MESH)
+            for side in (core, 1 - core) if beside else (core,):
+                pl.semaphore_signal(barrier, inc=1, device_id=(side, tile_of(shifted(pos, axis, by))), device_id_type=MESH)
     pl.semaphore_signal(barrier, inc=1, device_id=(1 - core, tile_of(pos)), device_id_type=MESH)
     if wait:
         greet_wait()
 
 
-def greet_wait():
-    pl.semaphore_wait(pltpu.get_barrier_semaphore(), 7)
+def greet_wait(count=7):
+    pl.semaphore_wait(pltpu.get_barrier_semaphore(), count)
 
 
 class Sender:
@@ -74,10 +75,10 @@
         self.pos, self.core, self.send_sem, self.recv_sem = pos, core, send_sem, recv_sem
         self.done = []
 
-    def copy(self, src, dst, sem, axis, by):
+    def copy(self, src, dst, sem, axis, by, core=None):
         c = pltpu.make_async_remote_copy(
             src_ref=src, dst_ref=dst, send_sem=self.send_sem.at[sem], recv_sem=self.recv_sem.at[sem],
-            device_id=(self.core, tile_of(shifted(self.pos, axis, by))), device_id_type=MESH)
+            device_id=(self.core if core is None else core, tile_of(shifted(self.pos, axis, by))), device_id_type=MESH)
         c.start()
         self.done.append(c)
         return c
@@ -105,55 +106,43 @@
 
 def forward_kernel(tok_ref, go_ref, wq_ref, wk_ref, wv_ref, wo_ref, kt_ref, kb_ref,
                    lay_ref, qp_ref, dop_ref, stat_ref, ent_ref, want_ref, inv_ref, rl_ref,
-                   mine, own, plane0, plane1, plane2, plane3, plane4, plane5, stage, arr0, arr1, arr2, arr3, e, kvb, qv, dov, stv, att, ng, lay,
+                   mine0, mine1, mine2, mine3, mine4, mine5, plane0, plane1, plane2, plane3, plane4, plane5, stage, arr0, arr1, arr2, arr3, e, kvb, qv, dov, stv, att, ng, lay,
                    named, ranks, tiles, wtab, itab, stab, want, slot,
-                   send_sem, recv_sem, swap_sem, local_sem, tab_sem, ent_sem, out_sem):
+                   send_sem, recv_sem, swap_sem, tab_sem, ent_sem, out_sem):
     pos, core = place(), lax.axis_index("vintage")
     me = tile_of(pos)
     planes, arr = ((plane0, plane1), (plane2, plane3), (plane4, plane5)), (arr0, arr1, arr2, arr3)
     dims = [tuple(sorted(o[:2])) for o in ORDERS]
     send = Sender(pos, core, send_sem, recv_sem)
     nb, L = 4, 16
-    greet(pos, core, False)
+    mine = ((mine0, mine1), (mine2, mine3), (mine4, mine5))
+    greet(pos, core, False, True)
 
     k = dot(tok_ref[...], wk_ref[...]).astype(BF16)
     v = dot(tok_ref[...], wv_ref[...]).astype(BF16)
     for g in range(4):
         both = jnp.concatenate([k[:, g * 64:g * 64 + 64], v[:, g * 64:g * 64 + 64]], axis=1)
-        for b in range(nb):
-            mine[b, g * 128:g * 128 + 128, :] = both[b * 128:b * 128 + 128]
-
-    greet_wait()
-    swap = pltpu.make_async_remote_copy(
-        src_ref=mine, dst_ref=own, send_sem=swap_sem.at[0], recv_sem=swap_sem.at[1],
-        device_id=(1 - core, me), device_id_type=MESH)
-    swap.start()
-
-    swap.wait()
+        for p in range(3):
+            r0, rows = spans(g)[p]
+            for b in range(nb):
+                mine[p][g // 2][b, offset(g, p):offset(g, p) + rows, :] = both[b * 128 + r0:b * 128 + r0 + rows]
+
+    greet_wait(13)
 
     def cell(p, h, a1, i1, a2, i2, *rest):
         return planes[p][h].at[tuple(i1 if d == a1 else i2 for d in dims[p]) + rest]
 
-    local = {}
-    for h in range(2):
-        for p in range(3):
-            a1, a2, a3 = ORDERS[p]
-            local[p, h] = []
-            for g in (2 * h, 2 * h + 1):
-                r0, rows = spans(g)[p]
-                c = pltpu.make_async_copy(own.at[:, pl.ds(g * 128 + r0, rows), :],
-                                          cell(p, h, a1, pos[a1], a2, pos[a2], slice(None), pl.ds(offset(g, p), rows), slice(None)),
-                                          local_sem.at[p * 4 + g])
-                c.start()
-                local[p, h].append(c)
-    first, second, third, fourth = {}, {}, {}, {}
+    first, second, third, fourth, swaps = {}, {}, {}, {}, {}
     pieces = [(p, h) for h in range(2) for p in range(3)]
     for p, h in pieces:
         a1, a2, a3 = ORDERS[p]
-        for c in local[p, h]:
-            c.wait()
         here = cell(p, h, a1, pos[a1], a2, pos[a2])
-        first[p, h] = [send.copy(here, here, (h * 3 + p) * 8 + i, a1, by) for i, by in enumerate((1, 3))]
+        first[p, h] = [send.copy(mine[p][h], here, (h * 3 + p) * 8 + i, a1, by, 1 - core) for i, by in enumerate((1, 3))]
+        c = pltpu.make_async_remote_copy(
+            src_ref=mine[p][h], dst_ref=here, send_sem=swap_sem.at[0, h * 3 + p], recv_sem=swap_sem.at[1, h * 3 + p],
+            device_id=(1 - core, me), device_id_type=MESH)
+        c.start()
+        swaps[p, h] = c
     kt, kb = kt_ref[...].T, kb_ref[...].T
     tiles[:, :L] = kt
     lane = lax.broadcasted_iota(jnp.int32, (256, 128), 1)
@@ -200,6 +189,7 @@
         a1, a2, a3 = ORDERS[p]
         for c in second[p, h]:
             c.wait_recv()
+        swaps[p, h].wait()
         here = planes[p][h].at[tuple(pos[a2] if d == a2 else slice(None) for d in dims[p])]
         third[p, h] = [send.copy(here, here, (h * 3 + p) * 8 + 4 + i, a2, by) for i, by in enumerate((1, 3))]
     zero = jnp.zeros((128, 64), BF16)
@@ -378,22 +368,22 @@
         out_specs=[A] * 8,
         out_shape=[bf(512, 768), bf(4, 4, 384, 128), bf(4, 4, 384, 128), jax.ShapeDtypeStruct((4, 4, 384, 128), F32),
                    bf(4, 64, 128, 128), i32(64, 128), i32(64, 128), bf(2, 2, 4, 2, 512, 128)],
-        scratch_shapes=[vm(4, 512, 128), vm(4, 512, 128)] + [
+        scratch_shapes=[vm(4, CUTS[2 * h][p] + CUTS[2 * h + 1][p], 128) for p in range(3) for h in range(2)] + [
             vm(4, 4, 4, CUTS[2 * h][p] + CUTS[2 * h + 1][p], 128) for p in range(3) for h in range(2)] + [
             vm(3, 4, 4, 2, 512, 128)] + [vm(4, 4, 4, 2, 128, 128)] * 4 + [pltpu.VMEM((384, 2048), F32), vm(2, 16, 128, 128),
             vm(4, 4, 384, 128), vm(4, 4, 384, 128), pltpu.VMEM((4, 4, 384, 128), F32), vm(4, 4, 384, 128),
             pltpu.VMEM((512, 768), F32), vm(512, 768),
             vi(256, 128), vi(256, 128), vi(256, 128), vi(64, 128), vi(64, 128), vi(8, 128),
             pltpu.SMEM((64, 128), jnp.int32), pltpu.SMEM((8, 128), jnp.int32),
-            dma(120), dma(120), dma(2), dma(12), dma(4), dma(2), dma(7)],
+            dma(120), dma(120), dma(2, 6), dma(4), dma(2), dma(7)],
         compiler_params=pltpu.CompilerParams(collective_id=0, has_side_effects=True, vmem_limit_bytes=67043328),
         name="forward",
     )(tokens, grads, w_query, w_key, w_value, w_out, named, blocks)
     return out[:7]
 
 
-def return_kernel(wanted, inv, qp_ref, dop_ref, stat_ref, ent_ref, wq_ref, wk_ref, wv_ref, out_ref, rl_ref, yl_ref, xl_ref,
-                  kvb, qv, dov, stv, p, t, dqs, parts, stage, rz, sums, gs, ys, hs, xs, total, got, wq, flat, wkv,
+def return_kernel(wanted, inv, qp_ref, dop_ref, stat_ref, ent_ref, wq_ref, wk_ref, wv_ref, out_ref, rl_ref,
+                  kvb, qv, dov, stv, p, t, dqs, parts, stage, rz, sums, gs, yl, ys, hs, xl, xs, total, got, wq, flat, wkv,
                   send_sem, recv_sem, swap_sem, kv_sem, in_sem, w_sem):
     pos, core = place(), lax.axis_index("vintage")
     dims = [tuple(sorted(o[:2])) for o in ORDERS]
@@ -469,7 +459,7 @@
             return 0
         lax.fori_loop(0, nb, one, 0)
 
-    zr, zd, zf, yr, yd, yf, xr, xd, xf = [{} for _ in range(9)]
+    zr, zd, zf, yr, yd, xr, xd = [{} for _ in range(7)]
 
     def slots_of(g, p, level, half=None):
         a3 = ORDERS[p][2]
@@ -573,37 +563,38 @@
             for c in zf[g][p * 2:p * 2 + 2]:
                 c.wait_recv()
             add_up(g, p, 2, 2, False, True)
-        for p in range(3):
-            a2 = ORDERS[p][1]
-            for i, by in enumerate((1, 3)):
-                yr[g].append(send.copy(lines(g, p, a2, turn(a2, 2), i), at_rows(yl_ref, g, p, (i, W, W)), key(g, p, 6 + i), a2, by))
-        for p in range(3):
-            a2 = ORDERS[p][1]
-            for i, by in enumerate((1, 3)):
-                yd[g].append(send.copy(lines(g, p, a2, turn(a2, by)), at_rows(ys, g, p, (i, W, W)), key(g, p, 8 + i), a2, by))
+            for i, by in enumerate((1, 3)):
+                yr[g].append(send.copy(lines(g, p, a2, turn(a2, 2), i), at_rows(yl, g, p, (i, W, W)), key(g, p, 6 + i), a2, by))
 
     def y_relay(g):
-        yf[g] = []
-        for p in range(3):
-            a2 = ORDERS[p][1]
-            for i, by in enumerate((1, 3)):
-                yr[g][p * 2 + i].wait_recv()
-                yf[g].append(send.copy(at_rows(yl_ref, g, p, (i, W, W)), at_rows(ys, g, p, (2, pl.ds(2 * i, 2), W)),
-                                       key(g, p, 10 + i), a2, by))
-
-    def x_send(g):
-        xr[g], xd[g] = [], []
         for p in range(3):
             a1, a2, a3 = ORDERS[p]
             r0, rows = spans(g)[p]
             at = (pl.ds(r0, rows), slice(None))
-            for c in yd[g][p * 2:p * 2 + 2] + yf[g][p * 2:p * 2 + 2]:
+            for i, by in enumerate((1, 3)):
+                yr[g][p * 2 + i].wait_recv()
+
+                def join(j, _, p=p, a1=a1, a2=a2, i=i, by=by, at=at):
+                    i1, b = lax.div(j, 4), lax.rem(j, 4)
+                    here = (g,) + tuple(2 * i + i1 if d == a1 else turn(a2, by) for d in dims[p]) + (b,) + at
+                    gs[here] = (gs[here].astype(F32) + yl[(g, i, i1, b) + at].astype(F32)).astype(BF16)
+                    return 0
+                lax.fori_loop(0, 8, join, 0)
+                yd[g].append(send.copy(lines(g, p, a2, turn(a2, by)), at_rows(ys, g, p, (i, W, W)), key(g, p, 8 + i), a2, by))
+
+    def x_send(g):
+        xr[g], xd[g] = [], []
+        for p in range(3):
+            a1, a2, a3 = ORDERS[p]
+            r0, rows = spans(g)[p]
+            at = (pl.ds(r0, rows), slice(None))
+            for c in yd[g][p * 2:p * 2 + 2]:
                 c.wait_recv()
 
             def row(j, _, p=p, a1=a1, a2=a2, at=at):
                 i1, b = lax.div(j, 4), lax.rem(j, 4)
                 mine = gs[(g,) + tuple(i1 if d == a1 else pos[a2] for d in dims[p]) + (b,) + at].astype(F32)
-                for k in range(3):
+                for k in range(2):
                     mine = mine + ys[(g, k, i1, b) + at].astype(F32)
                 hs[(g, i1, b) + at] = mine.astype(BF16)
                 return 0
@@ -611,33 +602,32 @@
         for p in range(3):
             a1 = ORDERS[p][0]
             for i, by in enumerate((1, 3)):
-                xr[g].append(send.copy(at_rows(hs, g, p, (turn(a1, 2), pl.ds(2 * i, 2))), at_rows(xl_ref, g, p, (i, W)), key(g, p, 12 + i), a1, by))
-        for p in range(3):
-            a1 = ORDERS[p][0]
-            for i, by in enumerate((1, 3)):
-                xd[g].append(send.copy(at_rows(hs, g, p, (turn(a1, by), W)), at_rows(xs, g, p, (i, W)), key(g, p, 14 + i), a1, by))
+                xr[g].append(send.copy(at_rows(hs, g, p, (turn(a1, 2), pl.ds(2 * i, 2))), at_rows(xl, g, p, (i, W)), key(g, p, 12 + i), a1, by))
 
     def x_relay(g):
-        xf[g] = []
-        for p in range(3):
-            a1 = ORDERS[p][0]
-            for i, by in enumerate((1, 3)):
-                xr[g][p * 2 + i].wait_recv()
-                xf[g].append(send.copy(at_rows(xl_ref, g, p, (i, W)), at_rows(xs, g, p, (2, pl.ds(2 * i, 2))),
-                                       key(g, p, 16 + i), a1, by))
-
-    swaps = []
-
-    def finish(g):
         for p in range(3):
             a1 = ORDERS[p][0]
             r0, rows = spans(g)[p]
             at = (pl.ds(r0, rows), slice(None))
-            for c in xd[g][p * 2:p * 2 + 2] + xf[g][p * 2:p * 2 + 2]:
+            for i, by in enumerate((1, 3)):
+                xr[g][p * 2 + i].wait_recv()
+                for b in range(2):
+                    here = (g, turn(a1, by), 2 * i + b) + at
+                    hs[here] = (hs[here].astype(F32) + xl[(g, i, b) + at].astype(F32)).astype(BF16)
+                xd[g].append(send.copy(at_rows(hs, g, p, (turn(a1, by), W)), at_rows(xs, g, p, (i, W)), key(g, p, 14 + i), a1, by))
+
+    swaps = []
+
+    def finish(g):
+        for p in range(3):
+            a1 = ORDERS[p][0]
+            r0, rows = spans(g)[p]
+            at = (pl.ds(r0, rows), slice(None))
+            for c in xd[g][p * 2:p * 2 + 2]:
                 c.wait_recv()
             for b in range(4):
                 mine = hs[(g, pos[a1], b) + at].astype(F32)
-                for k in range(3):
+                for k in range(2):
                     mine = mine + xs[(g, k, b) + at].astype(F32)
                 total[(g, b) + at] = mine.astype(BF16)
         c = pltpu.make_async_remote_copy(
@@ -718,7 +708,7 @@
         c.wait()
     for g in range(4):
         late = zr[g] + zd[g] if g >= 2 else []
-        for c in late + zf[g] + yr[g] + yd[g] + yf[g] + xr[g] + xd[g] + xf[g]:
+        for c in late + zf[g] + yr[g] + yd[g] + xr[g] + xd[g]:
             c.wait_send()
 
 
@@ -730,14 +720,14 @@
     out = pl.pallas_call(
         return_kernel,
         in_specs=[S, S] + [A] * 7,
-        out_specs=[A] * 4,
-        out_shape=[bf(512, 768), bf(4, 2, 2, 4, 2, 128, 128), bf(4, 2, 2, 4, 128, 128), bf(4, 2, 2, 128, 128)],
+        out_specs=[A] * 2,
+        out_shape=[bf(512, 768), bf(4, 2, 2, 4, 2, 128, 128)],
         scratch_shapes=[
             vm(2, 16, 128, 128), vm(4, 2, 384, 128), vm(4, 2, 384, 128), pltpu.VMEM((4, 2, 384, 128), F32),
             pltpu.VMEM((384, 2048), F32), pltpu.VMEM((384, 2048), F32), vm(4, 4, 384, 128),
             vm(64, 128, 128), vm(2, 4, 4, 4, 2, 128, 128), vm(4, 3, 4, 4, 2, 128, 128),
-            pltpu.VMEM((4, 4, 4, 128, 128), F32), vm(4, 4, 4, 4, 128, 128), vm(4, 3, 4, 4, 128, 128),
-            vm(4, 4, 4, 128, 128), vm(4, 3, 4, 128, 128), vm(4, 4, 128, 128), vm(4, 4, 128, 128),
+            pltpu.VMEM((4, 4, 4, 128, 128), F32), vm(4, 4, 4, 4, 128, 128), vm(4, 2, 2, 4, 128, 128), vm(4, 2, 4, 4, 128, 128),
+            vm(4, 4, 4, 128, 128), vm(4, 2, 2, 128, 128), vm(4, 2, 4, 128, 128), vm(4, 4, 128, 128), vm(4, 4, 128, 128),
             vm(768, 768), vm(1536, 256), vm(768, 512),
             pltpu.SemaphoreType.DMA((216,)), pltpu.SemaphoreType.DMA((216,)), pltpu.SemaphoreType.DMA((2, 4)),
             pltpu.SemaphoreType.DMA((2,)), pltpu.SemaphoreType.DMA((4, 3)), pltpu.SemaphoreType.DMA((6,))],

time: 262 us -> 256 us (0.977)
  Pallas kernels: 258 us -> 250 us
    pallas_call x1, Pallas kernels: 132 us -> 126 us  [gather_back(): pl.pallas_call(return_kernel, in_specs=[S, S] + [A] * 7, out_specs=[A] *...]
where the time goes in v5:
time: 256 us; the launch traced here: 255 us
  Pallas kernels  250 us (98%)
  local copies, waits for them, and re-layouts  4.13 us (2%)
    pallas_call x1, Pallas kernels, gather_back(): pl.pallas_call(return_kernel, in_specs=[S, S] + [A] * 7, out_specs=[A] *...  126 us
    pallas_call x1, Pallas kernels, forward_pass(): pl.pallas_call(forward_kernel, in_specs=[V] * 8, out_specs=[A] * 8, out_s...  124 us

profile of v5, /device:TPU:1, one launch (start us, length us, event | category | flops | bytes accessed | tf_op | source)
XLA Modules:
  0.0 255.2 jit_solution(1906742033519198367)
XLA Ops:
  0.6 124.5 %forward.1 = (bf16[512,768]{1,0:T(8,128)(2,1)}, bf16[4,4,384,128]{3,2,1,0:T(8,128)(2,1)}, bf16[4,4,384,128]{3,2,1,0:T(8,128)(2,1)}, f32[4,4,384,128]{3,2,1,0:T(8...) custom-call(bf16[512,768]{1,0:T(8,128)(2,1)} %bitcast.10, ...), custom_call_target="tpu_custom_call" | custom-call | tf_op jit(solution)/shard_map/forward/pallas_call | solution.py:365
  125.1 126.0 %collect.1 = (bf16[512,768]{1,0:T(8,128)(2,1)}, bf16[4,2,2,4,2,128,128]{6,5,4,3,2,1,0:T(8,128)(2,1)}) custom-call(s32[64,128]{1,0:T(8,128)} %get-tuple-element.11.wanted, s32[64,128]{1,0:T(8,128)} %get-tuple-element.12.inv, bf16[4,4,384,128]{3,2,1,0:T(8,128)(2,1)} %get-tuple-element.13.qp_ref, bf16[4,4,384,128]{3,2,1,0:T(8,128)(2,1)} %get-tuple-element.14.dop_ref, ...), custom_call_target="tpu_custom_call" | custom-call | tf_op jit(solution)/shard_map/collect/pallas_call | solution.py:720
  251.1 2.1 copy.12
  253.2 2.1 copy.13

commit v6 on v5

--- a/solution.py
+++ b/solution.py
@@ -319,14 +319,14 @@
     z_send(2)
     z_own(1)
     z_relay(1)
+    forward(0)
+    z_relay(2)
     z_send(3)
-    forward(0)
     z_own(2)
-    z_relay(2)
+    z_own(3)
     forward(1)
-    z_own(3)
+    forward(2)
     z_relay(3)
-    forward(2)
     forward(3)
 
     for b in range(nb):
@@ -658,17 +658,17 @@
     backward(0)
     z_send(0)
     backward(1)
+    z_relay(0)
     z_send(1)
-    z_relay(0)
     z_sum(0)
     backward(2)
+    z_relay(1)
     z_send(2)
-    z_relay(1)
     y_send(0)
     z_sum(1)
     backward(3)
+    z_relay(2)
     z_send(3)
-    z_relay(2)
     y_send(1)
     y_relay(0)
     z_sum(2)
@@ -737,10 +737,23 @@
     return out[0]
 
 
+def finish_kernel(layer_ref, total_ref, layer_out, total_out):
+    layer_out[...] = layer_ref[...]
+    total_out[...] = total_ref[...]
+
+
+def finish(layer, total):
+    block = pl.BlockSpec((256, 768), lambda i: (i, 0))
+    shape = jax.ShapeDtypeStruct((512, 768), BF16)
+    return pl.pallas_call(finish_kernel, grid=(2,), in_specs=[block] * 2, out_specs=[block] * 2, out_shape=[shape] * 2,
+                          name="finish")(layer, total)
+
+
 def shards(patches, out_grad, w_query, w_key, w_value, w_out, key_tiles, key_blocks):
     layer, qp, dop, stat, ent, wanted, inv = forward_pass(
         patches[0], out_grad[0], w_query, w_key, w_value, w_out, key_tiles[0].T, key_blocks[0].T)
     total = gather_back(wanted, inv, qp, dop, stat, ent, w_query, w_key, w_value)
+    layer, total = finish(layer, total)
     return layer[None], total[None]
 
 

time: 256 us -> 254 us (level)
  local copies, waits for them, and re-layouts: 4.13 us -> 0 us
  Pallas kernels: 250 us -> 253 us
    unnamed x2 -> x0, local copies, waits for them, and re-layouts: 4.13 us -> none
where the time goes in v6:
time: 254 us; the launch traced here: 253 us
  Pallas kernels  253 us (100%)
    pallas_call x1, Pallas kernels, forward_pass(): pl.pallas_call(forward_kernel, in_specs=[V] * 8, out_specs=[A] * 8, out_s...  126 us
    pallas_call x1, Pallas kernels, gather_back(): pl.pallas_call(return_kernel, in_specs=[S, S] + [A] * 7, out_specs=[A] *...  124 us

profile of v6, /device:TPU:1, one launch (start us, length us, event | category | flops | bytes accessed | tf_op | source)
XLA Modules:
  0.0 253.4 jit_solution(5742774419620270034)
XLA Ops:
  0.6 126.5 %forward.1 = (bf16[512,768]{1,0:T(8,128)(2,1)}, bf16[4,4,384,128]{3,2,1,0:T(8,128)(2,1)}, bf16[4,4,384,128]{3,2,1,0:T(8,128)(2,1)}, f32[4,4,384,128]{3,2,1,0:T(8...) custom-call(bf16[512,768]{1,0:T(8,128)(2,1)} %bitcast.10, ...), custom_call_target="tpu_custom_call" | custom-call | tf_op jit(solution)/shard_map/forward/pallas_call | solution.py:365
  127.1 123.9 %collect.1 = (bf16[512,768]{1,0:T(8,128)(2,1)}, bf16[4,2,2,4,2,128,128]{6,5,4,3,2,1,0:T(8,128)(2,1)}) custom-call(s32[64,128]{1,0:T(8,128)} %get-tuple-element.13.wanted, s32[64,128]{1,0:T(8,128)} %get-tuple-element.14.inv, bf16[4,4,384,128]{3,2,1,0:T(8,128)(2,1)} %get-tuple-element.15.qp_ref, bf16[4,4,384,128]{3,2,1,0:T(8,128)(2,1)} %get-tuple-element.16.dop_ref, ...), custom_call_target="tpu_custom_call" | custom-call | tf_op jit(solution)/shard_map/collect/pallas_call | solution.py:720
  251.1 2.3 finish.1
